TPU v7x, 256 devices: a whole 4x4x8 slice. The times are simulated.
256 devices in a mesh: blk: 32 (over y_lo, z, core), grp: 8 (over y_hi, x).
Axes of the slice: x: 4, y: 4 (y_hi: 2, y_lo: 2; y = y_hi * 2 + y_lo), z: 8, core: 2. Of those that a mesh axis runs over, the one named last changes fastest.
Arguments:
- orbitals: float32 [16384, 512], P('blk'), may hold values from -6 to 6
- points: float32 [3, 16384], P(None, 'blk'), may hold values from 0 to 1
Outputs:
- exchange_vectors: float32 [16384, 512], P('blk')
All inputs are finite; a program needn't handle non-finite values.
Results may differ from a plain program's by a relative error of at most 0.0003.
Values sent between devices are 32-bit elements; how exact they have to be, the bound alone decides.
No kernel may reach another device: no remote copies, remote signals or barrier semaphores. Data moves between devices by JAX's collectives and lax.ppermute only.
A program may use at most 64 MiB of HBM per device.

v0:
```python
import functools

import jax
import jax.numpy as jnp
from jax import lax
from jax.experimental import pallas as pl
from jax.experimental.pallas import tpu as pltpu
from jax.sharding import Mesh, PartitionSpec as P


HIGHEST = lax.Precision.HIGHEST
PLANE = ("x", "yh", "yl")

SIDE = 128


def lanes(value, index):
    return jnp.broadcast_to(value[:, index : index + 1], (8, SIDE))


def base(a_ref, z_ref, spread):
    strips = SIDE // 8
    lane = lax.broadcasted_iota(jnp.int32, (8, SIDE), 1)

    def opened(strip, block):
        start = 8 * strip
        inside = (lane >= start) & (lane < start + 8)
        for k in range(8):
            spread[8 * k : 8 * k + 8, :] = lanes(block, start + k)
        p = [[None] * 8 for _ in range(8)]
        for i in range(8):
            for k in range(i + 1):
                p[i][k] = p[k][i] = jnp.broadcast_to(spread[8 * k + i : 8 * k + i + 1, :], (8, SIDE))
        row = [jnp.broadcast_to(a_ref[start + i : start + i + 1, :], (8, SIDE)) for i in range(8)]
        row = [jnp.where(inside, jnp.where(lane == start + i, 1.0, 0.0), row[i]) for i in range(8)]
        return start, inside, row, p

    def update(strip, later, inside, row):
        there = slice(8 * later, 8 * later + 8)
        block = a_ref[there, :]
        product = [lanes(block, 8 * strip + k) * row[k] for k in range(8)]
        while len(product) > 1:
            product = [product[i] + product[i + 1] for i in range(0, len(product), 2)]
        block = jnp.where(inside, 0.0, block) - product[0]
        a_ref[there, :] = block
        return block

    state = opened(0, a_ref[:8, :])
    for strip in range(strips):
        start, inside, row, p = state
        for k in range(8):
            inv = 1.0 / p[k][k]
            z_ref[start + k : start + k + 1, :] = (row[k] * lax.rsqrt(p[k][k]))[:1]
            scaled = [None if i == k else p[i][k] * inv for i in range(8)]
            for i in list(range(k + 1, 8)) + list(range(k)):
                for l in range(k + 1, 8):
                    if i > k and l > i:
                        continue
                    if i == l == k + 1:
                        p[i][l] = p[i][l] - (p[i][k] * p[k][l]) * inv
                    else:
                        p[i][l] = p[i][l] - scaled[i] * p[k][l]
                    if i > k:
                        p[l][i] = p[i][l]
            for l in range(k + 1, 8):
                p[k][l] = scaled[l] if l > k else p[k][l]
            for i in range(8):
                if i != k:
                    row[i] = row[i] - scaled[i] * row[k]
            row[k] = row[k] * inv
        if strip + 1 < strips:
            state = opened(strip + 1, update(strip, strip + 1, inside, row))
        for later in range(strip + 2, strips):
            update(strip, later, inside, row)


def dot(a, b, dims, precision=HIGHEST):
    return lax.dot_general(a, b, (dims, ((), ())), precision=precision, preferred_element_type=jnp.float32)


def split(value):
    upper = value.astype(jnp.bfloat16)
    return upper, (value - upper.astype(jnp.float32)).astype(jnp.bfloat16)


def chol_kernel(core_ref, mine_ref, other_ref, z_ref, rows, base_a, base_z, spread):
    n = z_ref.shape[0]
    count = n // SIDE
    where = [(i, j) for i in range(count) for j in range(i, count)]
    each = len(where) // 2
    for number, (i, j) in enumerate(where):
        here = slice(number % each * SIDE, number % each * SIDE + SIDE)
        block = jnp.where(core_ref[0] == number // each, mine_ref[here, :], other_ref[here, :])
        z_ref[i * SIDE : i * SIDE + SIDE, j * SIDE : j * SIDE + SIDE] = block
        if i < j:
            z_ref[j * SIDE : j * SIDE + SIDE, i * SIDE : i * SIDE + SIDE] = jnp.zeros((SIDE, SIDE), jnp.float32)
    row = lax.broadcasted_iota(jnp.int32, (SIDE, SIDE), 0)
    column = lax.broadcasted_iota(jnp.int32, (SIDE, SIDE), 1)
    eye = jnp.where(row == column, 1.0, 0.0)

    def step(index, carry):
        here = pl.ds(pl.multiple_of(index * SIDE, SIDE), SIDE)
        base_a[...] = z_ref[here, here]
        base(base_a, base_z, spread)
        z_ref[here, here] = eye
        lower = jnp.where(row >= column, base_z[...], 0.0)
        rows[...] = dot(lower, z_ref[here, :], ((1,), (0,)))
        z_ref[here, :] = rows[...]

        def update(later, inner):
            there = pl.ds(pl.multiple_of(later * SIDE, SIDE), SIDE)
            z_ref[there, here] = jnp.zeros((SIDE, SIDE), jnp.float32)
            z_ref[there, :] = z_ref[there, :] - dot(rows[:, there], rows[...], ((0,), (0,)))
            return inner

        lax.fori_loop(index + 1, count, update, 0)
        return carry

    lax.fori_loop(0, count, step, 0)
    for i in range(count):
        for j in range(i + 1, count):
            z_ref[i * SIDE : i * SIDE + SIDE, j * SIDE : j * SIDE + SIDE] = jnp.zeros((SIDE, SIDE), jnp.float32)


def call(body, out_shape, scratch, aliases, flops, scalars, *operands):
    vmem = pl.BlockSpec(memory_space=pltpu.VMEM)
    smem = pl.BlockSpec(memory_space=pltpu.SMEM)
    return pl.pallas_call(
        body,
        out_shape=out_shape,
        in_specs=[smem] * scalars + [vmem] * (len(operands) - scalars),
        out_specs=jax.tree.map(lambda _: vmem, out_shape),
        scratch_shapes=scratch,
        input_output_aliases=aliases,
        cost_estimate=pl.CostEstimate(flops=flops, transcendentals=0, bytes_accessed=2 * 10**6),
    )(*operands)


def chol_inverse(core, mine, other, n):
    scratch = [pltpu.VMEM(s, jnp.float32) for s in ((SIDE, n), (SIDE, SIDE), (SIDE, SIDE), (64, SIDE))]
    return call(chol_kernel, jax.ShapeDtypeStruct((n, n), jnp.float32), scratch, {}, 2 * 10**10, 1, core, mine, other)


def near_kernel(own_ref, points_ref, below_ref, above_ref, near_ref, turned_ref, spread_ref):
    rows, orbs = own_ref.shape
    middle = rows // 2
    tall = 2 * rows
    parts = [
        (0, rows, own_ref, points_ref, 0),
        (rows, middle, below_ref, below_ref, middle),
        (rows + middle, middle, above_ref, above_ref, middle),
    ]
    for start, size, ref, coords, first in parts:
        for at in range(0, size, middle):
            value = ref[at : at + middle, :]
            there = slice(start + at, start + at + middle)
            upper, lower = split(value)
            near_ref[there, :orbs] = upper
            near_ref[there, orbs : 2 * orbs] = upper
            near_ref[there, 2 * orbs :] = lower
            upper, lower = split(value.T)
            for place, half in enumerate((upper, upper, lower)):
                turned_ref[:, place * tall + start + at : place * tall + start + at + middle] = half
            for k in range(3):
                line = coords[first + k : first + k + 1, at : at + middle]
                spread_ref[k, there, :] = jnp.broadcast_to(line, (SIDE, middle)).T


def add_tile(near_ref, spread_ref, acc, out, pieces, wide_far, tall_far, slab):
    chunk = pieces[0].shape[0] - 8
    orbs = out.shape[1]
    width = len(pieces) * chunk
    lane = lax.broadcasted_iota(jnp.int32, (8, SIDE), 1)
    for number, piece in enumerate(pieces):
        upper, lower = split(piece[:chunk, :])
        here = slice(number * chunk, number * chunk + chunk)
        for place, half in enumerate((upper, lower, upper)):
            wide_far[here, place * orbs : place * orbs + orbs] = half
            tall_far[place * width + number * chunk : place * width + number * chunk + chunk, :] = half
    for number in range(0, len(pieces), 2):
        left, right = (pieces[number + i][chunk : chunk + 8, :SIDE] for i in range(2))
        at = number * chunk
        slab[:, at : at + SIDE] = jnp.where(lane < chunk, left, pltpu.roll(right, chunk, 1))
    step = out.shape[0]
    for index in range(out.shape[0] // step):
        here = slice(index * step, index * step + step)
        gram = dot(near_ref[here, :], wide_far[...], ((1,), (1,)), None)
        squares = []
        for at in range(0, width, SIDE):
            square = 0.0025
            for k in range(3):
                spacing = spread_ref[k, here, :] - slab[k : k + 1, at : at + SIDE]
                square = square + spacing * spacing
            squares.append(square)
        upper, lower = split(gram * lax.rsqrt(jnp.concatenate(squares, axis=1)))
        product = dot(jnp.concatenate([upper, upper, lower], axis=1), tall_far[...], ((1,), (0,)), None)
        out[here, :] = product if acc is None else acc[here, :] + product


def first_kernel(pieces, *refs):
    found, out, scratch = refs[2 : 2 + pieces], refs[2 + pieces], refs[3 + pieces :]
    add_tile(*refs[:2], None, out, found, *scratch)


def tile_kernel(pieces, *refs):
    acc, found, out, scratch = refs[2], refs[3 : 3 + pieces], refs[3 + pieces], refs[4 + pieces :]
    add_tile(*refs[:2], acc, out, found, *scratch)


def last_kernel(pieces, weight, core_ref, near_ref, spread_ref, turned_ref, acc, *refs):
    found = refs[:pieces]
    own_ref, below_ref, above_ref, mine_ref, other_ref, total, halves = refs[pieces : 7 + pieces]
    add_tile(near_ref, spread_ref, acc, total, found, *refs[7 + pieces :])
    rows = own_ref.shape[0]
    middle = rows // 2
    tall = 2 * rows
    own_ref[...] = total[:rows, :] * weight
    below_ref[...] = total[rows : rows + middle, :] * weight
    above_ref[...] = total[rows + middle :, :] * weight
    upper, lower = split(total[...])
    for place, half in enumerate((upper, lower, upper)):
        halves[place * tall : place * tall + tall, :] = half
    count = total.shape[1] // SIDE
    number = 0
    each = count * (count + 1) // 4
    for i in range(count):
        left = turned_ref[i * SIDE : i * SIDE + SIDE, :]
        wide = dot(left, halves[:, i * SIDE :], ((1,), (0,)), None) * (weight * weight)
        for j in range(i, count):
            block = wide[:, (j - i) * SIDE : (j - i) * SIDE + SIDE]
            there = slice(number % each * SIDE, number % each * SIDE + SIDE)

            @pl.when(core_ref[0] == number // each)
            def _():
                mine_ref[there, :] = block

            @pl.when(core_ref[0] != number // each)
            def _():
                other_ref[there, :] = block

            number += 1


def scratch(pieces, chunk, orbs):
    wide = pieces * chunk
    return [
        pltpu.VMEM((wide, 3 * orbs), jnp.bfloat16),
        pltpu.VMEM((3 * wide, orbs), jnp.bfloat16),
        pltpu.VMEM((8, wide), jnp.float32),
    ]


def shift(block, axis, distance):
    size = lax.axis_size(axis)
    return lax.ppermute(block, axis, [(i, (i + distance) % size) for i in range(size)])


def shift_y(block, distance):
    size = lax.axis_size(("yl", "yh"))
    place = [(y % 2) * (size // 2) + y // 2 for y in range(size)]
    return lax.ppermute(block, ("yl", "yh"), [(place[y], place[(y + distance) % size]) for y in range(size)])


def gathered(piece, axes):
    copies = jnp.broadcast_to(piece[None], (lax.axis_size(axes),) + piece.shape)
    return lax.all_to_all(copies, axes, 0, 0, tiled=True)


def scattered_sum(parts, axes):
    return jnp.sum(lax.all_to_all(parts, axes, 0, 0, tiled=True), axis=0)


def packed(rows, coords):
    return jnp.concatenate([rows, jnp.pad(coords, ((0, 5), (0, rows.shape[1] - coords.shape[1])))], axis=0)


def shards(orbitals, points):
    rows, orbs = orbitals.shape
    core = lax.axis_index("c")
    core_ref = core.astype(jnp.int32)[None]
    groups = lax.axis_size(("yh", "x"))
    group = lax.axis_index(("yh", "x"))
    chunk = rows // groups
    weight = 1.0 / (rows * lax.axis_size(("yl", "z", "c")))
    barrier = lax.optimization_barrier

    own = packed(
        lax.dynamic_slice_in_dim(orbitals, group * chunk, chunk, 0),
        lax.dynamic_slice_in_dim(points, group * chunk, chunk, 1),
    )
    middle = rows // 2
    from_below = shift_y(packed(orbitals[:middle], points[:, :middle]), 1)
    from_above = shift_y(packed(orbitals[middle:], points[:, middle:]), -1)
    far = {0: own}
    ring = lax.axis_size("z")
    order = [0]
    for distance in range(1, ring // 2):
        order += [distance, -distance]
    order.append(ring // 2)
    for distance in order[1:]:
        far[distance] = shift(own, "z", distance)

    tall = 2 * rows
    near_type = jax.ShapeDtypeStruct((tall, 3 * orbs), jnp.bfloat16)
    turned_type = jax.ShapeDtypeStruct((orbs, 3 * tall), jnp.bfloat16)
    spread_type = jax.ShapeDtypeStruct((3, tall, SIDE), jnp.float32)
    near, turned, spread = call(
        near_kernel, (near_type, turned_type, spread_type), [], {}, 10**9, 0, orbitals, points, from_below, from_above
    )
    total_type = jax.ShapeDtypeStruct((tall, orbs), jnp.float32)
    stages = [order[:3], order[3:5], order[5:7], order[7:]]
    total = None
    for number, stage in enumerate(stages):
        pieces = []
        for distance in stage:
            pieces += [far[distance], shift(far[distance], "c", 1)]
        count = len(pieces)
        if number == 0:
            body = functools.partial(first_kernel, count)
            total = call(body, total_type, scratch(count, chunk, orbs), {}, 4 * 10**9, 0, near, spread, *pieces)
        elif number < len(stages) - 1:
            body = functools.partial(tile_kernel, count)
            total = call(body, total_type, scratch(count, chunk, orbs), {2: 0}, 3 * 10**9, 0, near, spread, total, *pieces)
    tri = (orbs // SIDE) * (orbs // SIDE + 1) // 4 * SIDE
    middle_type = jax.ShapeDtypeStruct((middle, orbs), jnp.float32)
    tri_type = jax.ShapeDtypeStruct((tri, SIDE), jnp.float32)
    own_part, to_above, to_below, mine, other = call(
        functools.partial(last_kernel, count, weight),
        (jax.ShapeDtypeStruct((rows, orbs), jnp.float32), middle_type, middle_type, tri_type, tri_type),
        [pltpu.VMEM((tall, orbs), jnp.float32), pltpu.VMEM((3 * tall, orbs), jnp.bfloat16)] + scratch(count, chunk, orbs),
        {}, 3 * 10**9, 1, core_ref, near, spread, turned, total, *pieces,
    )

    half = mine + shift(other, "c", 1)
    to_above = shift_y(to_above, 1)
    to_below = shift_y(to_below, -1)
    plane = lax.axis_size(PLANE)
    piece = scattered_sum(half.reshape(plane, -1, SIDE), PLANE)
    piece, to_above, to_below = barrier((piece, to_above, to_below))

    applied = own_part + jnp.concatenate([to_above, to_below], axis=0)
    lines = lax.axis_size("x")
    line, yh = lax.axis_index("x"), lax.axis_index("yh")
    by_line = applied.reshape(groups // lines, lines, chunk, orbs)
    parts = [lax.dynamic_index_in_dim(by_line, line, 1, keepdims=False)]
    for distance in range(1, lines):
        part = lax.dynamic_index_in_dim(by_line, (line + distance) % lines, 1, keepdims=False)
        parts.append(shift(part, "x", distance))
    piece = jnp.sum(gathered(piece, "z"), axis=0)
    pair = sum(parts[1:], parts[0])
    kept = lax.dynamic_index_in_dim(pair, yh, 0, keepdims=False)
    sent = shift(lax.dynamic_index_in_dim(pair, 1 - yh, 0, keepdims=False), "yh", 1)

    half = gathered(piece, PLANE).reshape(-1, SIDE)
    half, kept, sent = barrier((half, kept, sent))
    applied = kept + sent
    far_half, applied = barrier((shift(half, "c", 1), applied))
    applied = gathered(applied, ("yh", "x")).reshape(rows, orbs)
    inverse = chol_inverse(core_ref, half, far_half, orbs)
    return -dot(applied, inverse, ((1,), (1,)))


def solution(mesh):
    fine = Mesh(mesh.devices.reshape(2, 8, 2, 2, 4), ("yl", "z", "c", "yh", "x"))
    blk = ("yl", "z", "c")

    return jax.shard_map(
        shards,
        mesh=fine,
        in_specs=(P(blk, None), P(None, blk)),
        out_specs=P(blk, None),
        check_vma=False,
    )
```

profile of v0, /device:TPU:1, one launch (start us, length us, event | category | flops | bytes accessed | tf_op | source)
XLA Modules:
  0.0 165.6 jit_solution(18089844145109609287)
XLA Ops:
  1.4 2.2 %collective-permute-start = (f32[264,512]{1,0:T(8,128)S(1)}, f32[264,512]{1,0:T(8,128)S(1)}, u32[]{:S(2)}, u32[]{:S(2)}) collective-permute-start(f32[264,512]{1,0:T(8,128)S(1)} %select_maximum_fusion.1), channel_id=1, source_target_pairs={{0,128},{128,4},{4,132},{132,0},{1,129},{129,5},{5,133},{133,1},{2... | collective-permute-start | bytes 1622024 | tf_op jit(solution)/shard_map/ppermute | solution.py:261
  7.9 4.0 %collective-permute-start.5 = (f32[72,512]{1,0:T(8,128)S(1)}, f32[72,512]{1,0:T(8,128)S(1)}, u32[]{:S(2)}, u32[]{:S(2)}) collective-permute-start(f32[72,512]{1,0:T(8,128)S(1)} %select_maximum_fusion.2.refs_2_), channel_id=1, source_target_pairs={{0,112},{16,0},{32,16},{48,32},{64,48},{80,64},{96,80},{112,96},{1... | collective-permute-start | bytes 442376 | tf_op jit(solution)/shard_map/ppermute | solution.py:255
  17.2 1.9 %collective-permute-start.11 = (f32[72,512]{1,0:T(8,128)S(1)}, f32[72,512]{1,0:T(8,128)S(1)}, u32[]{:S(2)}, u32[]{:S(2)}) collective-permute-start(f32[72,512]{1,0:T(8,128)S(1)} %select_maximum_fusion.2.refs_2_), channel_id=1, source_target_pairs={{0,48},{16,64},{32,80},{48,96},{64,112},{80,0},{96,16},{112,32},{1... | collective-permute-start | bytes 442376 | tf_op jit(solution)/shard_map/ppermute | solution.py:255
  19.1 4.5 %collective-permute-done.9.refs_5_ = f32[72,512]{1,0:T(8,128)S(1)} collective-permute-done((f32[72,512]{1,0:T(8,128)S(1)}, f32[72,512]{1,0:T(8,128)S(1)}, u32[]{:S(2)}, u32[]{:S(2)}) %collective-permute-start.9) | collective-permute-done | bytes 147488 | tf_op jit(solution)/shard_map/ppermute | solution.py:255
  24.9 1.9 %collective-permute-start.15 = (f32[72,512]{1,0:T(8,128)S(1)}, f32[72,512]{1,0:T(8,128)S(1)}, u32[]{:S(2)}, u32[]{:S(2)}) collective-permute-start(f32[72,512]{1,0:T(8,128)S(1)} %select_maximum_fusion.2.refs_2_), channel_id=1, source_target_pairs={{0,64},{16,80},{32,96},{48,112},{64,0},{80,16},{96,32},{112,48},{1... | collective-permute-start | bytes 442376 | tf_op jit(solution)/shard_map/ppermute | solution.py:255
  26.9 12.5 %collective-permute-start.4 = (f32[72,512]{1,0:T(8,128)S(1)}, f32[72,512]{1,0:T(8,128)S(1)}, u32[]{:S(2)}, u32[]{:S(2)}) collective-permute-start(f32[72,512]{1,0:T(8,128)S(1)} %collective-permute-done.3.refs_4_), channel_id=1, source_target_pairs={{0,8},{8,0},{1,9},{9,1},{2,10},{10,2},{3,11},{11,3},{4,12},{12,4},... | collective-permute-start | bytes 442376 | tf_op jit(solution)/shard_map/ppermute | solution.py:255
  40.2 5.7 %shard_map.28 = (bf16[1024,1536]{1,0:T(8,128)(2,1)}, bf16[512,3072]{1,0:T(8,128)(2,1)}, f32[3,1024,128]{2,1,0:T(8,128)}) custom-call(f32[512,512]{1,0:T(8,128)} %own_ref.1, f32[3,512]{1,0:T(4,128)} %points_ref.1, f32[264,512]{1,0:T(8,128)} %copy-done.4, f32[264,512]{1,0:T(8,128)} %copy-done.5), custom_call_target="tpu_custom_call" | custom-call | flops 1000000000 | bytes 2000000 | tf_op jit(solution)/shard_map/pallas_call | solution.py:128
  47.6 7.4 %shard_map.29.refs_2_ = f32[1024,512]{1,0:T(8,128)} custom-call(bf16[1024,1536]{1,0:T(8,128)(2,1)} %get-tuple-element.21.refs_0_.near_ref, f32[3,1024,128]{2,1,0:T(8,128)} %get-tuple-element.22.refs_1_.spread_ref, f32[72,512]{1,0:T(8,128)} %copy-done.2, f32[72,512]{1,0:T(8,128)} %copy-done.12, f32[72,512]{1,0:T(8,128)} %copy-done.7, f32[72,512]{1,0:T(8,128)} %copy-done.15, ...), custom_call_target="tpu_custom_call" | custom-call | flops 4000000000 | bytes 2000000 | tf_op jit(solution)/shard_map/pallas_call | solution.py:128
  56.3 7.8 %shard_map.30.refs_2_ = f32[1024,512]{1,0:T(8,128)} custom-call(bf16[1024,1536]{1,0:T(8,128)(2,1)} %get-tuple-element.21.refs_0_.near_ref, f32[3,1024,128]{2,1,0:T(8,128)} %get-tuple-element.22.refs_1_.spread_ref, f32[1024,512]{1,0:T(8,128)} %shard_map.29.refs_2_, f32[72,512]{1,0:T(8,128)} %copy-done.13, ...), custom_call_target="tpu_custom_call", output_to_operand_aliasing={{}: (2, {})} | custom-call | flops 3000000000 | bytes 2000000 | tf_op jit(solution)/shard_map/pallas_call | solution.py:128
  65.5 7.8 %shard_map.31.acc = f32[1024,512]{1,0:T(8,128)} custom-call(bf16[1024,1536]{1,0:T(8,128)(2,1)} %get-tuple-element.21.refs_0_.near_ref, f32[3,1024,128]{2,1,0:T(8,128)} %get-tuple-element.22.refs_1_.spread_ref, f32[1024,512]{1,0:T(8,128)} %shard_map.30.refs_2_, f32[72,512]{1,0:T(8,128)} %copy-done.11, ...), custom_call_target="tpu_custom_call", output_to_operand_aliasing={{}: (2, {})} | custom-call | flops 3000000000 | bytes 2000000 | tf_op jit(solution)/shard_map/pallas_call | solution.py:128
  74.0 10.9 %shard_map.32 = (f32[512,512]{1,0:T(8,128)}, f32[256,512]{1,0:T(8,128)}, f32[256,512]{1,0:T(8,128)}, f32[640,128]{1,0:T(8,128)}, f32[640,128]{1,0:T(8,128)}) custom-call(s32[1]{0:T(128)} %bitcast.core_ref, bf16[1024,1536]{1,0:T(8,128)(2,1)} %get-tuple-element.21.refs_0_.near_ref, f32[3,1024,128]{2,1,0:T(8,128)} %get-tuple-element.22.refs_1_.spread_ref, ...), custom_call_target="tpu_custom_call" | custom-call | flops 3000000000 | bytes 2000000 | tf_op jit(solution)/shard_map/pallas_call | solution.py:128
  87.8 1.7 %add.73 = f32[640,128]{1,0:T(8,128)} add(f32[640,128]{1,0:T(8,128)} %get-tuple-element.24, f32[640,128]{1,0:T(8,128)S(1)} %collective-permute-done.17) | non-fusion elementwise | flops 81920 | bytes 983040 | tf_op jit(solution)/shard_map/add | solution.py:334
  89.5 5.6 %all-to-all-start = ((f32[16,40,128]{2,1,0:T(8,128)}), f32[16,40,128]{2,1,0:T(8,128)S(1)}, u32[]{:S(2)}, u32[]{:S(2)}) async-start(f32[16,40,128]{2,1,0:T(8,128)} %bitcast.1), calls=%async_computation | async-start | bytes 655360 | tf_op jit(solution)/shard_map/all_to_all | solution.py:270
  95.2 7.8 %all-to-all-done = f32[16,40,128]{2,1,0:T(8,128)S(1)} async-done(((f32[16,40,128]{2,1,0:T(8,128)}), f32[16,40,128]{2,1,0:T(8,128)S(1)}, u32[]{:S(2)}, u32[]{:S(2)}) %all-to-all-start) | async-done | bytes 327712 | tf_op jit(solution)/shard_map/all_to_all | solution.py:270
  103.7 3.4 %all-to-all-start.1 = ((f32[8,40,128]{2,1,0:T(8,128)}), f32[8,40,128]{2,1,0:T(8,128)S(1)}, u32[]{:S(2)}, u32[]{:S(2)}) async-start(f32[8,40,128]{2,1,0:T(8,128)} %broadcast_in_dim.9), calls=%async_computation.1 | async-start | bytes 327680 | tf_op jit(solution)/shard_map/all_to_all | solution.py:266
  108.7 2.4 %collective-permute-start.21 = (f32[2,64,512]{2,1,0:T(8,128)S(1)}, f32[2,64,512]{2,1,0:T(8,128)S(1)}, u32[]{:S(2)}, u32[]{:S(2)}) collective-permute-start(f32[2,64,512]{2,1,0:T(8,128)S(1)} %get-tuple-element.39), channel_id=1, source_target_pairs={{0,2},{1,3},{2,0},{3,1},{4,6},{5,7},{6,4},{7,5},{8,10},{9,11},{10,... | collective-permute-start | bytes 786440 | tf_op jit(solution)/shard_map/ppermute | solution.py:255
  112.3 3.0 %all-to-all-done.1 = f32[8,40,128]{2,1,0:T(8,128)S(1)} async-done(((f32[8,40,128]{2,1,0:T(8,128)}), f32[8,40,128]{2,1,0:T(8,128)S(1)}, u32[]{:S(2)}, u32[]{:S(2)}) %all-to-all-start.1) | async-done | bytes 163872 | tf_op jit(solution)/shard_map/all_to_all | solution.py:266
  116.1 6.4 %all-to-all-start.2 = ((f32[16,40,128]{2,1,0:T(8,128)}), f32[16,40,128]{2,1,0:T(8,128)S(1)}, u32[]{:S(2)}, u32[]{:S(2)}) async-start(f32[16,40,128]{2,1,0:T(8,128)} %broadcast_in_dim.10), calls=%async_computation.2 | async-start | bytes 655360 | tf_op jit(solution)/shard_map/all_to_all | solution.py:266
  122.7 3.0 %collective-permute-start.23 = (f32[64,512]{1,0:T(8,128)S(1)}, f32[64,512]{1,0:T(8,128)S(1)}, u32[]{:S(2)}, u32[]{:S(2)}) collective-permute-start(f32[64,512]{1,0:T(8,128)S(1)} %get-tuple-element.42), channel_id=1, source_target_pairs={{0,4},{4,0},{1,5},{5,1},{2,6},{6,2},{3,7},{7,3},{8,12},{12,8},{9,1... | collective-permute-start | bytes 393224 | tf_op jit(solution)/shard_map/ppermute | solution.py:255
  125.7 3.1 %collective-permute-done.23 = f32[64,512]{1,0:T(8,128)S(1)} collective-permute-done((f32[64,512]{1,0:T(8,128)S(1)}, f32[64,512]{1,0:T(8,128)S(1)}, u32[]{:S(2)}, u32[]{:S(2)}) %collective-permute-start.23) | collective-permute-done | bytes 131104 | tf_op jit(solution)/shard_map/ppermute | solution.py:255
  130.3 4.3 %collective-permute-start.24 = (f32[640,128]{1,0:T(8,128)S(1)}, f32[640,128]{1,0:T(8,128)S(1)}, u32[]{:S(2)}, u32[]{:S(2)}) collective-permute-start(f32[640,128]{1,0:T(8,128)S(1)} %bitcast.26), channel_id=1, source_target_pairs={{0,8},{8,0},{1,9},{9,1},{2,10},{10,2},{3,11},{11,3},{4,12},{12,4},... | collective-permute-start | bytes 983048 | tf_op jit(solution)/shard_map/ppermute | solution.py:255
  136.9 4.7 %all-to-all-start.3 = ((f32[8,64,512]{2,1,0:T(8,128)}), f32[8,64,512]{2,1,0:T(8,128)S(1)}, u32[]{:S(2)}, u32[]{:S(2)}) async-start(f32[8,64,512]{2,1,0:T(8,128)} %broadcast_in_dim.11), calls=%async_computation.3 | async-start | bytes 2097152 | tf_op jit(solution)/shard_map/all_to_all | solution.py:266
  141.6 19.9 %shard_map.33 = f32[512,512]{1,0:T(8,128)} custom-call(s32[1]{0:T(128)} %bitcast.core_ref, f32[640,128]{1,0:T(8,128)} %bitcast.27, f32[640,128]{1,0:T(8,128)} %copy-done.6), custom_call_target="tpu_custom_call" | custom-call | flops 20000000000 | bytes 2000000 | tf_op jit(solution)/shard_map/pallas_call | solution.py:128
  161.6 4.1 %convolution_negate_fusion = f32[512,512]{1,0:T(8,128)} fusion(f32[512,512]{1,0:T(8,128)S(1)} %bitcast.25, f32[512,512]{1,0:T(8,128)} %shard_map.33), kind=kOutput, calls=%fused_computation | convolution fusion | flops 1610874880 | bytes 3145728 | tf_op jit(solution)/shard_map/dot_general | solution.py:78
  (103 shorter events, 29.2 us)
Async XLA Ops:
  1.4 25.5 %collective-permute-start = (f32[264,512]{1,0:T(8,128)S(1)}, f32[264,512]{1,0:T(8,128)S(1)}, u32[]{:S(2)}, u32[]{:S(2)}) collective-permute-start(f32[264,512]{1,0:T(8,128)S(1)} %select_maximum_fusion.1), channel_id=1, source_target_pairs={{0,128},{128,4},{4,132},{132,0},{1,129},{129,5},{5,133},{133,1},{2... | collective-permute-start | bytes 1622024 | tf_op jit(solution)/shard_map/ppermute | solution.py:261
  3.6 35.8 %collective-permute-start.1 = (f32[264,512]{1,0:T(8,128)S(1)}, f32[264,512]{1,0:T(8,128)S(1)}, u32[]{:S(2)}, u32[]{:S(2)}) collective-permute-start(f32[264,512]{1,0:T(8,128)S(1)} %select_maximum_fusion), channel_id=1, source_target_pairs={{0,132},{128,0},{4,128},{132,4},{1,133},{129,1},{5,129},{133,5},{2... | collective-permute-start | bytes 1622024 | tf_op jit(solution)/shard_map/ppermute | solution.py:261
  6.1 8.7 %collective-permute-start.3 = (f32[72,512]{1,0:T(8,128)S(1)}, f32[72,512]{1,0:T(8,128)S(1)}, u32[]{:S(2)}, u32[]{:S(2)}) collective-permute-start(f32[72,512]{1,0:T(8,128)S(1)} %select_maximum_fusion.2.refs_2_), channel_id=1, source_target_pairs={{0,16},{16,32},{32,48},{48,64},{64,80},{80,96},{96,112},{112,0},{1... | collective-permute-start | bytes 442376 | tf_op jit(solution)/shard_map/ppermute | solution.py:255
  7.9 8.7 %collective-permute-start.5 = (f32[72,512]{1,0:T(8,128)S(1)}, f32[72,512]{1,0:T(8,128)S(1)}, u32[]{:S(2)}, u32[]{:S(2)}) collective-permute-start(f32[72,512]{1,0:T(8,128)S(1)} %select_maximum_fusion.2.refs_2_), channel_id=1, source_target_pairs={{0,112},{16,0},{32,16},{48,32},{64,48},{80,64},{96,80},{112,96},{1... | collective-permute-start | bytes 442376 | tf_op jit(solution)/shard_map/ppermute | solution.py:255
  14.9 8.7 %collective-permute-start.9 = (f32[72,512]{1,0:T(8,128)S(1)}, f32[72,512]{1,0:T(8,128)S(1)}, u32[]{:S(2)}, u32[]{:S(2)}) collective-permute-start(f32[72,512]{1,0:T(8,128)S(1)} %select_maximum_fusion.2.refs_2_), channel_id=1, source_target_pairs={{0,96},{16,112},{32,0},{48,16},{64,32},{80,48},{96,64},{112,80},{1... | collective-permute-start | bytes 442376 | tf_op jit(solution)/shard_map/ppermute | solution.py:255
  16.5 8.4 %collective-permute-start.7 = (f32[72,512]{1,0:T(8,128)S(1)}, f32[72,512]{1,0:T(8,128)S(1)}, u32[]{:S(2)}, u32[]{:S(2)}) collective-permute-start(f32[72,512]{1,0:T(8,128)S(1)} %select_maximum_fusion.2.refs_2_), channel_id=1, source_target_pairs={{0,32},{16,48},{32,64},{48,80},{64,96},{80,112},{96,0},{112,16},{1... | collective-permute-start | bytes 442376 | tf_op jit(solution)/shard_map/ppermute | solution.py:255
  17.2 28.6 %collective-permute-start.11 = (f32[72,512]{1,0:T(8,128)S(1)}, f32[72,512]{1,0:T(8,128)S(1)}, u32[]{:S(2)}, u32[]{:S(2)}) collective-permute-start(f32[72,512]{1,0:T(8,128)S(1)} %select_maximum_fusion.2.refs_2_), channel_id=1, source_target_pairs={{0,48},{16,64},{32,80},{48,96},{64,112},{80,0},{96,16},{112,32},{1... | collective-permute-start | bytes 442376 | tf_op jit(solution)/shard_map/ppermute | solution.py:255
  23.6 22.5 %collective-permute-start.13 = (f32[72,512]{1,0:T(8,128)S(1)}, f32[72,512]{1,0:T(8,128)S(1)}, u32[]{:S(2)}, u32[]{:S(2)}) collective-permute-start(f32[72,512]{1,0:T(8,128)S(1)} %select_maximum_fusion.2.refs_2_), channel_id=1, source_target_pairs={{0,80},{16,96},{32,112},{48,0},{64,16},{80,32},{96,48},{112,64},{1... | collective-permute-start | bytes 442376 | tf_op jit(solution)/shard_map/ppermute | solution.py:255
  24.9 21.5 %collective-permute-start.15 = (f32[72,512]{1,0:T(8,128)S(1)}, f32[72,512]{1,0:T(8,128)S(1)}, u32[]{:S(2)}, u32[]{:S(2)}) collective-permute-start(f32[72,512]{1,0:T(8,128)S(1)} %select_maximum_fusion.2.refs_2_), channel_id=1, source_target_pairs={{0,64},{16,80},{32,96},{48,112},{64,0},{80,16},{96,32},{112,48},{1... | collective-permute-start | bytes 442376 | tf_op jit(solution)/shard_map/ppermute | solution.py:255
  26.9 19.7 %collective-permute-start.4 = (f32[72,512]{1,0:T(8,128)S(1)}, f32[72,512]{1,0:T(8,128)S(1)}, u32[]{:S(2)}, u32[]{:S(2)}) collective-permute-start(f32[72,512]{1,0:T(8,128)S(1)} %collective-permute-done.3.refs_4_), channel_id=1, source_target_pairs={{0,8},{8,0},{1,9},{9,1},{2,10},{10,2},{3,11},{11,3},{4,12},{12,4},... | collective-permute-start | bytes 442376 | tf_op jit(solution)/shard_map/ppermute | solution.py:255
  45.9 9.1 %collective-permute-start.10 = (f32[72,512]{1,0:T(8,128)S(1)}, f32[72,512]{1,0:T(8,128)S(1)}, u32[]{:S(2)}, u32[]{:S(2)}) collective-permute-start(f32[72,512]{1,0:T(8,128)S(1)} %collective-permute-done.9.refs_5_), channel_id=1, source_target_pairs={{0,8},{8,0},{1,9},{9,1},{2,10},{10,2},{3,11},{11,3},{4,12},{12,4},... | collective-permute-start | bytes 442376 | tf_op jit(solution)/shard_map/ppermute | solution.py:255
  46.1 9.0 %collective-permute-start.8 = (f32[72,512]{1,0:T(8,128)S(1)}, f32[72,512]{1,0:T(8,128)S(1)}, u32[]{:S(2)}, u32[]{:S(2)}) collective-permute-start(f32[72,512]{1,0:T(8,128)S(1)} %collective-permute-done.7.refs_3_), channel_id=1, source_target_pairs={{0,8},{8,0},{1,9},{9,1},{2,10},{10,2},{3,11},{11,3},{4,12},{12,4},... | collective-permute-start | bytes 442376 | tf_op jit(solution)/shard_map/ppermute | solution.py:255
  46.4 17.8 %collective-permute-start.12 = (f32[72,512]{1,0:T(8,128)S(1)}, f32[72,512]{1,0:T(8,128)S(1)}, u32[]{:S(2)}, u32[]{:S(2)}) collective-permute-start(f32[72,512]{1,0:T(8,128)S(1)} %collective-permute-done.11.refs_3_), channel_id=1, source_target_pairs={{0,8},{8,0},{1,9},{9,1},{2,10},{10,2},{3,11},{11,3},{4,12},{12,4},... | collective-permute-start | bytes 442376 | tf_op jit(solution)/shard_map/ppermute | solution.py:255
  46.6 17.6 %collective-permute-start.14 = (f32[72,512]{1,0:T(8,128)S(1)}, f32[72,512]{1,0:T(8,128)S(1)}, u32[]{:S(2)}, u32[]{:S(2)}) collective-permute-start(f32[72,512]{1,0:T(8,128)S(1)} %collective-permute-done.13.refs_5_), channel_id=1, source_target_pairs={{0,8},{8,0},{1,9},{9,1},{2,10},{10,2},{3,11},{11,3},{4,12},{12,4},... | collective-permute-start | bytes 442376 | tf_op jit(solution)/shard_map/ppermute | solution.py:255
  46.9 26.5 %collective-permute-start.16 = (f32[72,512]{1,0:T(8,128)S(1)}, f32[72,512]{1,0:T(8,128)S(1)}, u32[]{:S(2)}, u32[]{:S(2)}) collective-permute-start(f32[72,512]{1,0:T(8,128)S(1)} %collective-permute-done.15.refs_0_), channel_id=1, source_target_pairs={{0,8},{8,0},{1,9},{9,1},{2,10},{10,2},{3,11},{11,3},{4,12},{12,4},... | collective-permute-start | bytes 442376 | tf_op jit(solution)/shard_map/ppermute | solution.py:255
  85.1 17.9 %collective-permute-start.18 = (f32[256,512]{1,0:T(8,128)}, f32[256,512]{1,0:T(8,128)S(1)}, u32[]{:S(2)}, u32[]{:S(2)}) collective-permute-start(f32[256,512]{1,0:T(8,128)} %get-tuple-element.26), channel_id=1, source_target_pairs={{0,128},{128,4},{4,132},{132,0},{1,129},{129,5},{5,133},{133,1},{2... | collective-permute-start | bytes 1572872 | tf_op jit(solution)/shard_map/ppermute | solution.py:261
  86.2 16.8 %collective-permute-start.19 = (f32[256,512]{1,0:T(8,128)}, f32[256,512]{1,0:T(8,128)S(1)}, u32[]{:S(2)}, u32[]{:S(2)}) collective-permute-start(f32[256,512]{1,0:T(8,128)} %get-tuple-element.27), channel_id=1, source_target_pairs={{0,132},{128,0},{4,128},{132,4},{1,133},{129,1},{5,129},{133,5},{2... | collective-permute-start | bytes 1572872 | tf_op jit(solution)/shard_map/ppermute | solution.py:261
  89.5 13.4 %all-to-all-start = ((f32[16,40,128]{2,1,0:T(8,128)}), f32[16,40,128]{2,1,0:T(8,128)S(1)}, u32[]{:S(2)}, u32[]{:S(2)}) async-start(f32[16,40,128]{2,1,0:T(8,128)} %bitcast.1), calls=%async_computation | async-start | bytes 655360 | tf_op jit(solution)/shard_map/all_to_all | solution.py:270
  103.7 11.7 %all-to-all-start.1 = ((f32[8,40,128]{2,1,0:T(8,128)}), f32[8,40,128]{2,1,0:T(8,128)S(1)}, u32[]{:S(2)}, u32[]{:S(2)}) async-start(f32[8,40,128]{2,1,0:T(8,128)} %broadcast_in_dim.9), calls=%async_computation.1 | async-start | bytes 327680 | tf_op jit(solution)/shard_map/all_to_all | solution.py:266
  107.4 15.2 %collective-permute-start.20 = (f32[2,64,512]{2,1,0:T(8,128)S(1)}, f32[2,64,512]{2,1,0:T(8,128)S(1)}, u32[]{:S(2)}, u32[]{:S(2)}) collective-permute-start(f32[2,64,512]{2,1,0:T(8,128)S(1)} %get-tuple-element.37), channel_id=1, source_target_pairs={{0,1},{1,2},{2,3},{3,0},{4,5},{5,6},{6,7},{7,4},{8,9},{9,10},{10,1... | collective-permute-start | bytes 786440 | tf_op jit(solution)/shard_map/ppermute | solution.py:255
  108.7 13.8 %collective-permute-start.21 = (f32[2,64,512]{2,1,0:T(8,128)S(1)}, f32[2,64,512]{2,1,0:T(8,128)S(1)}, u32[]{:S(2)}, u32[]{:S(2)}) collective-permute-start(f32[2,64,512]{2,1,0:T(8,128)S(1)} %get-tuple-element.39), channel_id=1, source_target_pairs={{0,2},{1,3},{2,0},{3,1},{4,6},{5,7},{6,4},{7,5},{8,10},{9,11},{10,... | collective-permute-start | bytes 786440 | tf_op jit(solution)/shard_map/ppermute | solution.py:255
  111.2 11.4 %collective-permute-start.22 = (f32[2,64,512]{2,1,0:T(8,128)S(1)}, f32[2,64,512]{2,1,0:T(8,128)S(1)}, u32[]{:S(2)}, u32[]{:S(2)}) collective-permute-start(f32[2,64,512]{2,1,0:T(8,128)S(1)} %get-tuple-element.38), channel_id=1, source_target_pairs={{0,3},{1,0},{2,1},{3,2},{4,7},{5,4},{6,5},{7,6},{8,11},{9,8},{10,9... | collective-permute-start | bytes 786440 | tf_op jit(solution)/shard_map/ppermute | solution.py:255
  116.1 14.1 %all-to-all-start.2 = ((f32[16,40,128]{2,1,0:T(8,128)}), f32[16,40,128]{2,1,0:T(8,128)S(1)}, u32[]{:S(2)}, u32[]{:S(2)}) async-start(f32[16,40,128]{2,1,0:T(8,128)} %broadcast_in_dim.10), calls=%async_computation.2 | async-start | bytes 655360 | tf_op jit(solution)/shard_map/all_to_all | solution.py:266
  136.9 24.7 %all-to-all-start.3 = ((f32[8,64,512]{2,1,0:T(8,128)}), f32[8,64,512]{2,1,0:T(8,128)S(1)}, u32[]{:S(2)}, u32[]{:S(2)}) async-start(f32[8,64,512]{2,1,0:T(8,128)} %broadcast_in_dim.11), calls=%async_computation.3 | async-start | bytes 2097152 | tf_op jit(solution)/shard_map/all_to_all | solution.py:266
  (27 other events, 308.2 us)
where the time goes:
time: 166 us
  starting transfers between devices  66.1 us (40%)
  Pallas kernels  59.6 us (36%)
  waiting for transfers between devices  24.1 us (15%)
  local copies, waits for them, and re-layouts  9.27 us (6%)
  matrix products  4.05 us (2%)
  other arithmetic  2.19 us (1%)
    pallas_call x6, Pallas kernels, call(): pl.pallas_call(body, out_shape=out_shape, in_specs=[smem] * scalars + [vm...  59.6 us
    ppermute x21, starting transfers between devices, shift(): lax.ppermute(block, axis, [(i, (i + distance) % size) for i in range(size)])  39.6 us
    all_to_all x3, starting transfers between devices, gathered(): return lax.all_to_all(copies, axes, 0, 0, tiled=True)  14.5 us
    ppermute x21, waiting for transfers between devices, shift(): lax.ppermute(block, axis, [(i, (i + distance) % size) for i in range(size)])  11.8 us
    all_to_all x1, waiting for transfers between devices, scattered_sum(): return jnp.sum(lax.all_to_all(parts, axes, 0, 0, tiled=True), axis=0)  7.8 us
    ppermute x4, starting transfers between devices, shift_y(): lax.ppermute(block, ('yl', 'yh'), [(place[y], place[(y + distance) % size...  6.4 us
    all_to_all x1, starting transfers between devices, scattered_sum(): return jnp.sum(lax.all_to_all(parts, axes, 0, 0, tiled=True), axis=0)  5.6 us
    all_to_all x3, waiting for transfers between devices, gathered(): return lax.all_to_all(copies, axes, 0, 0, tiled=True)  4.47 us
  transfers between devices with their start and end apart: 29, of which 8 were waited for; matrix products, arithmetic and copies ran while one was open for 2% of the time, Pallas kernels for 29%

commit v1 on v0

--- a/solution.py
+++ b/solution.py
@@ -133,6 +133,7 @@
         scratch_shapes=scratch,
         input_output_aliases=aliases,
         cost_estimate=pl.CostEstimate(flops=flops, transcendentals=0, bytes_accessed=2 * 10**6),
+        compiler_params=pltpu.CompilerParams(vmem_limit_bytes=16 * 2**20),
     )(*operands)
 
 
@@ -141,7 +142,7 @@
     return call(chol_kernel, jax.ShapeDtypeStruct((n, n), jnp.float32), scratch, {}, 2 * 10**10, 1, core, mine, other)
 
 
-def near_kernel(own_ref, points_ref, below_ref, above_ref, near_ref, turned_ref, spread_ref):
+def near_kernel(core_ref, line_ref, yh_ref, own_ref, points_ref, below_ref, above_ref, near_ref, turned_ref, spread_ref):
     rows, orbs = own_ref.shape
     middle = rows // 2
     tall = 2 * rows
@@ -277,7 +278,9 @@
 def shards(orbitals, points):
     rows, orbs = orbitals.shape
     core = lax.axis_index("c")
+    line, yh = lax.axis_index("x"), lax.axis_index("yh")
     core_ref = core.astype(jnp.int32)[None]
+    place = [core_ref, line.astype(jnp.int32)[None], yh.astype(jnp.int32)[None]]
     groups = lax.axis_size(("yh", "x"))
     group = lax.axis_index(("yh", "x"))
     chunk = rows // groups
@@ -305,7 +308,7 @@
     turned_type = jax.ShapeDtypeStruct((orbs, 3 * tall), jnp.bfloat16)
     spread_type = jax.ShapeDtypeStruct((3, tall, SIDE), jnp.float32)
     near, turned, spread = call(
-        near_kernel, (near_type, turned_type, spread_type), [], {}, 10**9, 0, orbitals, points, from_below, from_above
+        near_kernel, (near_type, turned_type, spread_type), [], {}, 10**9, 3, *place, orbitals, points, from_below, from_above
     )
     total_type = jax.ShapeDtypeStruct((tall, orbs), jnp.float32)
     stages = [order[:3], order[3:5], order[5:7], order[7:]]
@@ -340,7 +343,6 @@
 
     applied = own_part + jnp.concatenate([to_above, to_below], axis=0)
     lines = lax.axis_size("x")
-    line, yh = lax.axis_index("x"), lax.axis_index("yh")
     by_line = applied.reshape(groups // lines, lines, chunk, orbs)
     parts = [lax.dynamic_index_in_dim(by_line, line, 1, keepdims=False)]
     for distance in range(1, lines):

time: 166 us -> 142 us (0.86)
  Pallas kernels: 59.6 us -> 36.1 us
  local copies, waits for them, and re-layouts: 9.27 us -> 4.1 us
  starting transfers between devices: 66.1 us -> 70.1 us
  waiting for transfers between devices: 24.1 us -> 25.9 us
    pallas_call x6, Pallas kernels: 59.6 us -> 36.1 us  [call(): pl.pallas_call(body, out_shape=out_shape, in_specs=[smem] * scalars + [vm...]
    ppermute x21, starting transfers between devices: 39.6 us -> 44.7 us  [shift(): lax.ppermute(block, axis, [(i, (i + distance) % size) for i in range(size)])]
    unnamed x44 -> x4, local copies, waits for them, and re-layouts: 4.37 us -> 0.01 us
    all_to_all x1, waiting for transfers between devices: 7.8 us -> 10.1 us  [scattered_sum(): return jnp.sum(lax.all_to_all(parts, axes, 0, 0, tiled=True), axis=0)]
  transfers between devices with their start and end apart: 29 -> 29, of which waited for: 8 -> 8; matrix products, arithmetic and copies ran while one was open for 2% -> 2% of each run, Pallas kernels for 29% -> 21%
where the time goes in v1:
time: 142 us
  starting transfers between devices  70.1 us (49%)
  Pallas kernels  36.1 us (25%)
  waiting for transfers between devices  25.9 us (18%)
  local copies, waits for them, and re-layouts  4.1 us (3%)
  matrix products  2.83 us (2%)
  other arithmetic  2.8 us (2%)
    ppermute x21, starting transfers between devices, shift(): lax.ppermute(block, axis, [(i, (i + distance) % size) for i in range(size)])  44.7 us
    pallas_call x6, Pallas kernels, call(): pl.pallas_call(body, out_shape=out_shape, in_specs=[smem] * scalars + [vm...  36.1 us
    all_to_all x3, starting transfers between devices, gathered(): return lax.all_to_all(copies, axes, 0, 0, tiled=True)  15 us
    ppermute x21, waiting for transfers between devices, shift(): lax.ppermute(block, axis, [(i, (i + distance) % size) for i in range(size)])  11.6 us
    all_to_all x1, waiting for transfers between devices, scattered_sum(): return jnp.sum(lax.all_to_all(parts, axes, 0, 0, tiled=True), axis=0)  10.1 us
    ppermute x4, starting transfers between devices, shift_y(): lax.ppermute(block, ('yl', 'yh'), [(place[y], place[(y + distance) % size...  6.23 us
    all_to_all x3, waiting for transfers between devices, gathered(): return lax.all_to_all(copies, axes, 0, 0, tiled=True)  4.15 us
    all_to_all x1, starting transfers between devices, scattered_sum(): return jnp.sum(lax.all_to_all(parts, axes, 0, 0, tiled=True), axis=0)  4.13 us
  transfers between devices with their start and end apart: 29, of which 8 were waited for; matrix products, arithmetic and copies ran while one was open for 2% of the time, Pallas kernels for 21%

profile of v1, /device:TPU:1, one launch (start us, length us, event | category | flops | bytes accessed | tf_op | source)
XLA Modules:
  0.0 142.0 jit_solution(4563255735471618032)
XLA Ops:
  2.2 2.1 %collective-permute-start = (f32[264,512]{1,0:T(8,128)}, f32[264,512]{1,0:T(8,128)S(1)}, u32[]{:S(2)}, u32[]{:S(2)}) collective-permute-start(f32[264,512]{1,0:T(8,128)} %select_maximum_fusion.1), channel_id=1, source_target_pairs={{0,128},{128,4},{4,132},{132,0},{1,129},{129,5},{5,133},{133,1},{2... | collective-permute-start | bytes 1622024 | tf_op jit(solution)/shard_map/ppermute | solution.py:262
  8.5 4.0 %collective-permute-start.5 = (f32[72,512]{1,0:T(8,128)S(1)}, f32[72,512]{1,0:T(8,128)S(1)}, u32[]{:S(2)}, u32[]{:S(2)}) collective-permute-start(f32[72,512]{1,0:T(8,128)S(1)} %select_maximum_fusion.2.refs_2_), channel_id=1, source_target_pairs={{0,112},{16,0},{32,16},{48,32},{64,48},{80,64},{96,80},{112,96},{1... | collective-permute-start | bytes 442376 | tf_op jit(solution)/shard_map/ppermute | solution.py:256
  17.8 1.9 %collective-permute-start.11 = (f32[72,512]{1,0:T(8,128)S(1)}, f32[72,512]{1,0:T(8,128)S(1)}, u32[]{:S(2)}, u32[]{:S(2)}) collective-permute-start(f32[72,512]{1,0:T(8,128)S(1)} %select_maximum_fusion.2.refs_2_), channel_id=1, source_target_pairs={{0,48},{16,64},{32,80},{48,96},{64,112},{80,0},{96,16},{112,32},{1... | collective-permute-start | bytes 442376 | tf_op jit(solution)/shard_map/ppermute | solution.py:256
  19.7 4.5 %collective-permute-done.9.refs_5_ = f32[72,512]{1,0:T(8,128)S(1)} collective-permute-done((f32[72,512]{1,0:T(8,128)S(1)}, f32[72,512]{1,0:T(8,128)S(1)}, u32[]{:S(2)}, u32[]{:S(2)}) %collective-permute-start.9) | collective-permute-done | bytes 147488 | tf_op jit(solution)/shard_map/ppermute | solution.py:256
  25.4 2.0 %collective-permute-start.15 = (f32[72,512]{1,0:T(8,128)S(1)}, f32[72,512]{1,0:T(8,128)S(1)}, u32[]{:S(2)}, u32[]{:S(2)}) collective-permute-start(f32[72,512]{1,0:T(8,128)S(1)} %select_maximum_fusion.2.refs_2_), channel_id=1, source_target_pairs={{0,64},{16,80},{32,96},{48,112},{64,0},{80,16},{96,32},{112,48},{1... | collective-permute-start | bytes 442376 | tf_op jit(solution)/shard_map/ppermute | solution.py:256
  27.3 12.5 %collective-permute-start.4 = (f32[72,512]{1,0:T(8,128)S(1)}, f32[72,512]{1,0:T(8,128)}, u32[]{:S(2)}, u32[]{:S(2)}) collective-permute-start(f32[72,512]{1,0:T(8,128)S(1)} %collective-permute-done.3.refs_4_), channel_id=1, source_target_pairs={{0,8},{8,0},{1,9},{9,1},{2,10},{10,2},{3,11},{11,3},{4,12},{12,4},... | collective-permute-start | bytes 442376 | tf_op jit(solution)/shard_map/ppermute | solution.py:256
  41.8 4.5 %collective-permute-start.12 = (f32[72,512]{1,0:T(8,128)S(1)}, f32[72,512]{1,0:T(8,128)S(1)}, u32[]{:S(2)}, u32[]{:S(2)}) collective-permute-start(f32[72,512]{1,0:T(8,128)S(1)} %collective-permute-done.11.refs_3_), channel_id=1, source_target_pairs={{0,8},{8,0},{1,9},{9,1},{2,10},{10,2},{3,11},{11,3},{4,12},{12,4},... | collective-permute-start | bytes 442376 | tf_op jit(solution)/shard_map/ppermute | solution.py:256
  46.9 4.6 %shard_map.29.refs_2_ = f32[1024,512]{1,0:T(8,128)S(1)} custom-call(bf16[1024,1536]{1,0:T(8,128)(2,1)S(1)} %get-tuple-element.21.refs_0_.near_ref, f32[3,1024,128]{2,1,0:T(8,128)S(1)} %get-tuple-element.22.refs_1_.spread_ref, f32[72,512]{1,0:T(8,128)S(1)} %select_maximum_fusion.2.refs_2_, f32[72,512]{1,0:T(8,128)S(1)} %collective-permute-done.2.refs_3_, ...), custom_call_target="tpu_custom_call" | custom-call | flops 4000000000 | bytes 2000000 | tf_op jit(solution)/shard_map/pallas_call | solution.py:128
  51.5 3.4 %shard_map.30.refs_2_ = f32[1024,512]{1,0:T(8,128)S(1)} custom-call(bf16[1024,1536]{1,0:T(8,128)(2,1)S(1)} %get-tuple-element.21.refs_0_.near_ref, f32[3,1024,128]{2,1,0:T(8,128)S(1)} %get-tuple-element.22.refs_1_.spread_ref, f32[1024,512]{1,0:T(8,128)S(1)} %shard_map.29.refs_2_, ...), custom_call_target="tpu_custom_call", output_to_operand_aliasing={{}: (2, {})} | custom-call | flops 3000000000 | bytes 2000000 | tf_op jit(solution)/shard_map/pallas_call | solution.py:128
  55.0 3.4 %shard_map.31.acc = f32[1024,512]{1,0:T(8,128)S(1)} custom-call(bf16[1024,1536]{1,0:T(8,128)(2,1)S(1)} %get-tuple-element.21.refs_0_.near_ref, f32[3,1024,128]{2,1,0:T(8,128)S(1)} %get-tuple-element.22.refs_1_.spread_ref, f32[1024,512]{1,0:T(8,128)S(1)} %shard_map.30.refs_2_, ...), custom_call_target="tpu_custom_call", output_to_operand_aliasing={{}: (2, {})} | custom-call | flops 3000000000 | bytes 2000000 | tf_op jit(solution)/shard_map/pallas_call | solution.py:128
  58.5 5.6 %shard_map.32 = (f32[512,512]{1,0:T(8,128)S(1)}, f32[256,512]{1,0:T(8,128)S(1)}, f32[256,512]{1,0:T(8,128)S(1)}, f32[640,128]{1,0:T(8,128)S(1)}, f32[640,128]{1,0:T(8,128)S(1)}) custom-call(s32[1]{0:T(128)} %bitcast.core_ref, bf16[1024,1536]{1,0:T(8,128)(2,1)S(1)} %get-tuple-element.21.refs_0_.near_ref, ...), custom_call_target="tpu_custom_call" | custom-call | flops 3000000000 | bytes 2000000 | tf_op jit(solution)/shard_map/pallas_call | solution.py:128
  64.4 2.7 %collective-permute-start.19 = (f32[256,512]{1,0:T(8,128)S(1)}, f32[256,512]{1,0:T(8,128)S(1)}, u32[]{:S(2)}, u32[]{:S(2)}) collective-permute-start(f32[256,512]{1,0:T(8,128)S(1)} %get-tuple-element.27), channel_id=1, source_target_pairs={{0,132},{128,0},{4,128},{132,4},{1,133},{129,1},{5,129},{133,5},{2... | collective-permute-start | bytes 1572872 | tf_op jit(solution)/shard_map/ppermute | solution.py:262
  67.8 4.1 %all-to-all-start = ((f32[16,40,128]{2,1,0:T(8,128)}), f32[16,40,128]{2,1,0:T(8,128)S(1)}, u32[]{:S(2)}, u32[]{:S(2)}) async-start(f32[16,40,128]{2,1,0:T(8,128)} %bitcast.3), calls=%async_computation | async-start | bytes 655360 | tf_op jit(solution)/shard_map/all_to_all | solution.py:271
  72.0 10.1 %all-to-all-done = f32[16,40,128]{2,1,0:T(8,128)S(1)} async-done(((f32[16,40,128]{2,1,0:T(8,128)}), f32[16,40,128]{2,1,0:T(8,128)S(1)}, u32[]{:S(2)}, u32[]{:S(2)}) %all-to-all-start) | async-done | bytes 327712 | tf_op jit(solution)/shard_map/all_to_all | solution.py:271
  82.8 3.6 %all-to-all-start.1 = ((f32[8,40,128]{2,1,0:T(8,128)}), f32[8,40,128]{2,1,0:T(8,128)S(1)}, u32[]{:S(2)}, u32[]{:S(2)}) async-start(f32[8,40,128]{2,1,0:T(8,128)} %broadcast_in_dim.30), calls=%async_computation.1 | async-start | bytes 327680 | tf_op jit(solution)/shard_map/all_to_all | solution.py:267
  88.5 2.4 %collective-permute-start.21 = (f32[2,64,512]{2,1,0:T(8,128)S(1)}, f32[2,64,512]{2,1,0:T(8,128)S(1)}, u32[]{:S(2)}, u32[]{:S(2)}) collective-permute-start(f32[2,64,512]{2,1,0:T(8,128)S(1)} %get-tuple-element.39), channel_id=1, source_target_pairs={{0,2},{1,3},{2,0},{3,1},{4,6},{5,7},{6,4},{7,5},{8,10},{9,11},{10,... | collective-permute-start | bytes 786440 | tf_op jit(solution)/shard_map/ppermute | solution.py:256
  92.0 2.7 %all-to-all-done.1 = f32[8,40,128]{2,1,0:T(8,128)S(1)} async-done(((f32[8,40,128]{2,1,0:T(8,128)}), f32[8,40,128]{2,1,0:T(8,128)S(1)}, u32[]{:S(2)}, u32[]{:S(2)}) %all-to-all-start.1) | async-done | bytes 163872 | tf_op jit(solution)/shard_map/all_to_all | solution.py:267
  95.5 6.7 %all-to-all-start.2 = ((f32[16,40,128]{2,1,0:T(8,128)}), f32[16,40,128]{2,1,0:T(8,128)S(1)}, u32[]{:S(2)}, u32[]{:S(2)}) async-start(f32[16,40,128]{2,1,0:T(8,128)} %broadcast_in_dim.31), calls=%async_computation.2 | async-start | bytes 655360 | tf_op jit(solution)/shard_map/all_to_all | solution.py:267
  102.3 3.0 %collective-permute-start.23 = (f32[64,512]{1,0:T(8,128)S(1)}, f32[64,512]{1,0:T(8,128)S(1)}, u32[]{:S(2)}, u32[]{:S(2)}) collective-permute-start(f32[64,512]{1,0:T(8,128)S(1)} %get-tuple-element.42), channel_id=1, source_target_pairs={{0,4},{4,0},{1,5},{5,1},{2,6},{6,2},{3,7},{7,3},{8,12},{12,8},{9,1... | collective-permute-start | bytes 393224 | tf_op jit(solution)/shard_map/ppermute | solution.py:256
  105.3 3.1 %collective-permute-done.23 = f32[64,512]{1,0:T(8,128)S(1)} collective-permute-done((f32[64,512]{1,0:T(8,128)S(1)}, f32[64,512]{1,0:T(8,128)S(1)}, u32[]{:S(2)}, u32[]{:S(2)}) %collective-permute-start.23) | collective-permute-done | bytes 131104 | tf_op jit(solution)/shard_map/ppermute | solution.py:256
  109.9 4.4 %collective-permute-start.24 = (f32[640,128]{1,0:T(8,128)S(1)}, f32[640,128]{1,0:T(8,128)S(1)}, u32[]{:S(2)}, u32[]{:S(2)}) collective-permute-start(f32[640,128]{1,0:T(8,128)S(1)} %bitcast.25), channel_id=1, source_target_pairs={{0,8},{8,0},{1,9},{9,1},{2,10},{10,2},{3,11},{11,3},{4,12},{12,4},... | collective-permute-start | bytes 983048 | tf_op jit(solution)/shard_map/ppermute | solution.py:256
  116.6 4.7 %all-to-all-start.3 = ((f32[8,64,512]{2,1,0:T(8,128)}), f32[8,64,512]{2,1,0:T(8,128)S(1)}, u32[]{:S(2)}, u32[]{:S(2)}) async-start(f32[8,64,512]{2,1,0:T(8,128)} %broadcast_in_dim.32), calls=%async_computation.3 | async-start | bytes 2097152 | tf_op jit(solution)/shard_map/all_to_all | solution.py:267
  121.4 17.8 %shard_map.33 = f32[512,512]{1,0:T(8,128)S(1)} custom-call(s32[1]{0:T(128)} %bitcast.core_ref, f32[640,128]{1,0:T(8,128)S(1)} %bitcast.26, f32[640,128]{1,0:T(8,128)S(1)} %collective-permute-done.24.other_ref), custom_call_target="tpu_custom_call" | custom-call | flops 20000000000 | bytes 2000000 | tf_op jit(solution)/shard_map/pallas_call | solution.py:128
  139.2 2.8 %convolution_negate_fusion = f32[512,512]{1,0:T(8,128)} fusion(f32[512,512]{1,0:T(8,128)S(1)} %bitcast.29, f32[512,512]{1,0:T(8,128)S(1)} %shard_map.33), kind=kOutput, calls=%fused_computation | convolution fusion | flops 1610874880 | bytes 3145728 | tf_op jit(solution)/shard_map/dot_general | solution.py:78
  (63 shorter events, 25.0 us)
Async XLA Ops:
  2.2 25.1 %collective-permute-start = (f32[264,512]{1,0:T(8,128)}, f32[264,512]{1,0:T(8,128)S(1)}, u32[]{:S(2)}, u32[]{:S(2)}) collective-permute-start(f32[264,512]{1,0:T(8,128)} %select_maximum_fusion.1), channel_id=1, source_target_pairs={{0,128},{128,4},{4,132},{132,0},{1,129},{129,5},{5,133},{133,1},{2... | collective-permute-start | bytes 1622024 | tf_op jit(solution)/shard_map/ppermute | solution.py:262
  5.2 34.7 %collective-permute-start.1 = (f32[264,512]{1,0:T(8,128)}, f32[264,512]{1,0:T(8,128)S(1)}, u32[]{:S(2)}, u32[]{:S(2)}) collective-permute-start(f32[264,512]{1,0:T(8,128)} %select_maximum_fusion), channel_id=1, source_target_pairs={{0,132},{128,0},{4,128},{132,4},{1,133},{129,1},{5,129},{133,5},{2... | collective-permute-start | bytes 1622024 | tf_op jit(solution)/shard_map/ppermute | solution.py:262
  6.7 8.7 %collective-permute-start.3 = (f32[72,512]{1,0:T(8,128)S(1)}, f32[72,512]{1,0:T(8,128)S(1)}, u32[]{:S(2)}, u32[]{:S(2)}) collective-permute-start(f32[72,512]{1,0:T(8,128)S(1)} %select_maximum_fusion.2.refs_2_), channel_id=1, source_target_pairs={{0,16},{16,32},{32,48},{48,64},{64,80},{80,96},{96,112},{112,0},{1... | collective-permute-start | bytes 442376 | tf_op jit(solution)/shard_map/ppermute | solution.py:256
  8.5 8.7 %collective-permute-start.5 = (f32[72,512]{1,0:T(8,128)S(1)}, f32[72,512]{1,0:T(8,128)S(1)}, u32[]{:S(2)}, u32[]{:S(2)}) collective-permute-start(f32[72,512]{1,0:T(8,128)S(1)} %select_maximum_fusion.2.refs_2_), channel_id=1, source_target_pairs={{0,112},{16,0},{32,16},{48,32},{64,48},{80,64},{96,80},{112,96},{1... | collective-permute-start | bytes 442376 | tf_op jit(solution)/shard_map/ppermute | solution.py:256
  15.4 8.7 %collective-permute-start.9 = (f32[72,512]{1,0:T(8,128)S(1)}, f32[72,512]{1,0:T(8,128)S(1)}, u32[]{:S(2)}, u32[]{:S(2)}) collective-permute-start(f32[72,512]{1,0:T(8,128)S(1)} %select_maximum_fusion.2.refs_2_), channel_id=1, source_target_pairs={{0,96},{16,112},{32,0},{48,16},{64,32},{80,48},{96,64},{112,80},{1... | collective-permute-start | bytes 442376 | tf_op jit(solution)/shard_map/ppermute | solution.py:256
  17.1 8.3 %collective-permute-start.7 = (f32[72,512]{1,0:T(8,128)S(1)}, f32[72,512]{1,0:T(8,128)S(1)}, u32[]{:S(2)}, u32[]{:S(2)}) collective-permute-start(f32[72,512]{1,0:T(8,128)S(1)} %select_maximum_fusion.2.refs_2_), channel_id=1, source_target_pairs={{0,32},{16,48},{32,64},{48,80},{64,96},{80,112},{96,0},{112,16},{1... | collective-permute-start | bytes 442376 | tf_op jit(solution)/shard_map/ppermute | solution.py:256
  17.8 23.4 %collective-permute-start.11 = (f32[72,512]{1,0:T(8,128)S(1)}, f32[72,512]{1,0:T(8,128)S(1)}, u32[]{:S(2)}, u32[]{:S(2)}) collective-permute-start(f32[72,512]{1,0:T(8,128)S(1)} %select_maximum_fusion.2.refs_2_), channel_id=1, source_target_pairs={{0,48},{16,64},{32,80},{48,96},{64,112},{80,0},{96,16},{112,32},{1... | collective-permute-start | bytes 442376 | tf_op jit(solution)/shard_map/ppermute | solution.py:256
  24.2 17.5 %collective-permute-start.13 = (f32[72,512]{1,0:T(8,128)S(1)}, f32[72,512]{1,0:T(8,128)S(1)}, u32[]{:S(2)}, u32[]{:S(2)}) collective-permute-start(f32[72,512]{1,0:T(8,128)S(1)} %select_maximum_fusion.2.refs_2_), channel_id=1, source_target_pairs={{0,80},{16,96},{32,112},{48,0},{64,16},{80,32},{96,48},{112,64},{1... | collective-permute-start | bytes 442376 | tf_op jit(solution)/shard_map/ppermute | solution.py:256
  25.4 16.5 %collective-permute-start.15 = (f32[72,512]{1,0:T(8,128)S(1)}, f32[72,512]{1,0:T(8,128)S(1)}, u32[]{:S(2)}, u32[]{:S(2)}) collective-permute-start(f32[72,512]{1,0:T(8,128)S(1)} %select_maximum_fusion.2.refs_2_), channel_id=1, source_target_pairs={{0,64},{16,80},{32,96},{48,112},{64,0},{80,16},{96,32},{112,48},{1... | collective-permute-start | bytes 442376 | tf_op jit(solution)/shard_map/ppermute | solution.py:256
  27.3 19.0 %collective-permute-start.4 = (f32[72,512]{1,0:T(8,128)S(1)}, f32[72,512]{1,0:T(8,128)}, u32[]{:S(2)}, u32[]{:S(2)}) collective-permute-start(f32[72,512]{1,0:T(8,128)S(1)} %collective-permute-done.3.refs_4_), channel_id=1, source_target_pairs={{0,8},{8,0},{1,9},{9,1},{2,10},{10,2},{3,11},{11,3},{4,12},{12,4},... | collective-permute-start | bytes 442376 | tf_op jit(solution)/shard_map/ppermute | solution.py:256
  41.2 10.3 %collective-permute-start.10 = (f32[72,512]{1,0:T(8,128)S(1)}, f32[72,512]{1,0:T(8,128)S(1)}, u32[]{:S(2)}, u32[]{:S(2)}) collective-permute-start(f32[72,512]{1,0:T(8,128)S(1)} %collective-permute-done.9.refs_5_), channel_id=1, source_target_pairs={{0,8},{8,0},{1,9},{9,1},{2,10},{10,2},{3,11},{11,3},{4,12},{12,4},... | collective-permute-start | bytes 442376 | tf_op jit(solution)/shard_map/ppermute | solution.py:256
  41.7 9.8 %collective-permute-start.8 = (f32[72,512]{1,0:T(8,128)S(1)}, f32[72,512]{1,0:T(8,128)S(1)}, u32[]{:S(2)}, u32[]{:S(2)}) collective-permute-start(f32[72,512]{1,0:T(8,128)S(1)} %collective-permute-done.7.refs_3_), channel_id=1, source_target_pairs={{0,8},{8,0},{1,9},{9,1},{2,10},{10,2},{3,11},{11,3},{4,12},{12,4},... | collective-permute-start | bytes 442376 | tf_op jit(solution)/shard_map/ppermute | solution.py:256
  41.8 13.1 %collective-permute-start.12 = (f32[72,512]{1,0:T(8,128)S(1)}, f32[72,512]{1,0:T(8,128)S(1)}, u32[]{:S(2)}, u32[]{:S(2)}) collective-permute-start(f32[72,512]{1,0:T(8,128)S(1)} %collective-permute-done.11.refs_3_), channel_id=1, source_target_pairs={{0,8},{8,0},{1,9},{9,1},{2,10},{10,2},{3,11},{11,3},{4,12},{12,4},... | collective-permute-start | bytes 442376 | tf_op jit(solution)/shard_map/ppermute | solution.py:256
  46.4 8.6 %collective-permute-start.14 = (f32[72,512]{1,0:T(8,128)S(1)}, f32[72,512]{1,0:T(8,128)S(1)}, u32[]{:S(2)}, u32[]{:S(2)}) collective-permute-start(f32[72,512]{1,0:T(8,128)S(1)} %collective-permute-done.13.refs_5_), channel_id=1, source_target_pairs={{0,8},{8,0},{1,9},{9,1},{2,10},{10,2},{3,11},{11,3},{4,12},{12,4},... | collective-permute-start | bytes 442376 | tf_op jit(solution)/shard_map/ppermute | solution.py:256
  46.4 12.1 %collective-permute-start.16 = (f32[72,512]{1,0:T(8,128)S(1)}, f32[72,512]{1,0:T(8,128)S(1)}, u32[]{:S(2)}, u32[]{:S(2)}) collective-permute-start(f32[72,512]{1,0:T(8,128)S(1)} %collective-permute-done.15.refs_0_), channel_id=1, source_target_pairs={{0,8},{8,0},{1,9},{9,1},{2,10},{10,2},{3,11},{11,3},{4,12},{12,4},... | collective-permute-start | bytes 442376 | tf_op jit(solution)/shard_map/ppermute | solution.py:256
  64.4 17.8 %collective-permute-start.18 = (f32[256,512]{1,0:T(8,128)S(1)}, f32[256,512]{1,0:T(8,128)S(1)}, u32[]{:S(2)}, u32[]{:S(2)}) collective-permute-start(f32[256,512]{1,0:T(8,128)S(1)} %get-tuple-element.26), channel_id=1, source_target_pairs={{0,128},{128,4},{4,132},{132,0},{1,129},{129,5},{5,133},{133,1},{2... | collective-permute-start | bytes 1572872 | tf_op jit(solution)/shard_map/ppermute | solution.py:262
  64.4 17.8 %collective-permute-start.19 = (f32[256,512]{1,0:T(8,128)S(1)}, f32[256,512]{1,0:T(8,128)S(1)}, u32[]{:S(2)}, u32[]{:S(2)}) collective-permute-start(f32[256,512]{1,0:T(8,128)S(1)} %get-tuple-element.27), channel_id=1, source_target_pairs={{0,132},{128,0},{4,128},{132,4},{1,133},{129,1},{5,129},{133,5},{2... | collective-permute-start | bytes 1572872 | tf_op jit(solution)/shard_map/ppermute | solution.py:262
  67.8 14.3 %all-to-all-start = ((f32[16,40,128]{2,1,0:T(8,128)}), f32[16,40,128]{2,1,0:T(8,128)S(1)}, u32[]{:S(2)}, u32[]{:S(2)}) async-start(f32[16,40,128]{2,1,0:T(8,128)} %bitcast.3), calls=%async_computation | async-start | bytes 655360 | tf_op jit(solution)/shard_map/all_to_all | solution.py:271
  82.8 11.9 %all-to-all-start.1 = ((f32[8,40,128]{2,1,0:T(8,128)}), f32[8,40,128]{2,1,0:T(8,128)S(1)}, u32[]{:S(2)}, u32[]{:S(2)}) async-start(f32[8,40,128]{2,1,0:T(8,128)} %broadcast_in_dim.30), calls=%async_computation.1 | async-start | bytes 327680 | tf_op jit(solution)/shard_map/all_to_all | solution.py:267
  86.7 15.4 %collective-permute-start.20 = (f32[2,64,512]{2,1,0:T(8,128)S(1)}, f32[2,64,512]{2,1,0:T(8,128)S(1)}, u32[]{:S(2)}, u32[]{:S(2)}) collective-permute-start(f32[2,64,512]{2,1,0:T(8,128)S(1)} %get-tuple-element.37), channel_id=1, source_target_pairs={{0,1},{1,2},{2,3},{3,0},{4,5},{5,6},{6,7},{7,4},{8,9},{9,10},{10,1... | collective-permute-start | bytes 786440 | tf_op jit(solution)/shard_map/ppermute | solution.py:256
  88.5 13.7 %collective-permute-start.21 = (f32[2,64,512]{2,1,0:T(8,128)S(1)}, f32[2,64,512]{2,1,0:T(8,128)S(1)}, u32[]{:S(2)}, u32[]{:S(2)}) collective-permute-start(f32[2,64,512]{2,1,0:T(8,128)S(1)} %get-tuple-element.39), channel_id=1, source_target_pairs={{0,2},{1,3},{2,0},{3,1},{4,6},{5,7},{6,4},{7,5},{8,10},{9,11},{10,... | collective-permute-start | bytes 786440 | tf_op jit(solution)/shard_map/ppermute | solution.py:256
  90.9 11.3 %collective-permute-start.22 = (f32[2,64,512]{2,1,0:T(8,128)S(1)}, f32[2,64,512]{2,1,0:T(8,128)S(1)}, u32[]{:S(2)}, u32[]{:S(2)}) collective-permute-start(f32[2,64,512]{2,1,0:T(8,128)S(1)} %get-tuple-element.38), channel_id=1, source_target_pairs={{0,3},{1,0},{2,1},{3,2},{4,7},{5,4},{6,5},{7,6},{8,11},{9,8},{10,9... | collective-permute-start | bytes 786440 | tf_op jit(solution)/shard_map/ppermute | solution.py:256
  95.5 14.3 %all-to-all-start.2 = ((f32[16,40,128]{2,1,0:T(8,128)}), f32[16,40,128]{2,1,0:T(8,128)S(1)}, u32[]{:S(2)}, u32[]{:S(2)}) async-start(f32[16,40,128]{2,1,0:T(8,128)} %broadcast_in_dim.31), calls=%async_computation.2 | async-start | bytes 655360 | tf_op jit(solution)/shard_map/all_to_all | solution.py:267
  116.6 22.6 %all-to-all-start.3 = ((f32[8,64,512]{2,1,0:T(8,128)}), f32[8,64,512]{2,1,0:T(8,128)S(1)}, u32[]{:S(2)}, u32[]{:S(2)}) async-start(f32[8,64,512]{2,1,0:T(8,128)} %broadcast_in_dim.32), calls=%async_computation.3 | async-start | bytes 2097152 | tf_op jit(solution)/shard_map/all_to_all | solution.py:267
  (7 other events, 34.7 us)

commit v2 on v1

--- a/solution.py
+++ b/solution.py
@@ -142,29 +142,22 @@
     return call(chol_kernel, jax.ShapeDtypeStruct((n, n), jnp.float32), scratch, {}, 2 * 10**10, 1, core, mine, other)
 
 
-def near_kernel(core_ref, line_ref, yh_ref, own_ref, points_ref, below_ref, above_ref, near_ref, turned_ref, spread_ref):
-    rows, orbs = own_ref.shape
-    middle = rows // 2
-    tall = 2 * rows
-    parts = [
-        (0, rows, own_ref, points_ref, 0),
-        (rows, middle, below_ref, below_ref, middle),
-        (rows + middle, middle, above_ref, above_ref, middle),
-    ]
-    for start, size, ref, coords, first in parts:
-        for at in range(0, size, middle):
-            value = ref[at : at + middle, :]
-            there = slice(start + at, start + at + middle)
-            upper, lower = split(value)
-            near_ref[there, :orbs] = upper
-            near_ref[there, orbs : 2 * orbs] = upper
-            near_ref[there, 2 * orbs :] = lower
-            upper, lower = split(value.T)
-            for place, half in enumerate((upper, upper, lower)):
-                turned_ref[:, place * tall + start + at : place * tall + start + at + middle] = half
-            for k in range(3):
-                line = coords[first + k : first + k + 1, at : at + middle]
-                spread_ref[k, there, :] = jnp.broadcast_to(line, (SIDE, middle)).T
+def near_kernel(lower_ref, upper_ref, below_ref, above_ref, near_ref, turned_ref, spread_ref):
+    middle, orbs = lower_ref.shape[0] - 8, lower_ref.shape[1]
+    tall = near_ref.shape[0]
+    for part, ref in enumerate((lower_ref, upper_ref, below_ref, above_ref)):
+        there = slice(part * middle, part * middle + middle)
+        value = ref[:middle, :]
+        upper, lower = split(value)
+        near_ref[there, :orbs] = upper
+        near_ref[there, orbs : 2 * orbs] = upper
+        near_ref[there, 2 * orbs :] = lower
+        upper, lower = split(value.T)
+        for place, half in enumerate((upper, upper, lower)):
+            turned_ref[:, place * tall + part * middle : place * tall + part * middle + middle] = half
+        for k in range(3):
+            line = ref[middle + k : middle + k + 1, :middle]
+            spread_ref[k, there, :] = jnp.broadcast_to(line, (SIDE, middle)).T
 
 
 def add_tile(near_ref, spread_ref, acc, out, pieces, wide_far, tall_far, slab):
@@ -242,6 +235,54 @@
             number += 1
 
 
+def pack_kernel(group_ref, core_ref, line_ref, rows_ref, points_ref, own_ref, below_ref, above_ref):
+    chunk = own_ref.shape[0] - 8
+    rows, orbs = rows_ref.shape
+    middle = rows // 2
+    own_ref[:chunk, :] = rows_ref[pl.ds(pl.multiple_of(group_ref[0] * chunk, chunk), chunk), :]
+    for line in range(3):
+        turned = pltpu.roll(jnp.broadcast_to(points_ref[line : line + 1, :], (8, rows)), rows - group_ref[0] * chunk, 1)
+        own_ref[chunk + line : chunk + line + 1, :] = turned[:1, :orbs]
+    own_ref[chunk + 3 :, :] = jnp.zeros((5, orbs), jnp.float32)
+    for start, ref in ((0, below_ref), (middle, above_ref)):
+        ref[:middle, :] = rows_ref[start : start + middle, :]
+        ref[middle:, :] = jnp.zeros((8, orbs), jnp.float32)
+        ref[middle : middle + 3, :middle] = points_ref[:, start : start + middle]
+
+
+def mark_kernel(number_ref, out_ref):
+    out_ref[0] = number_ref[0]
+
+
+def mark(number):
+    smem = pl.BlockSpec(memory_space=pltpu.SMEM)
+    out_shape = jax.ShapeDtypeStruct((1,), jnp.int32)
+    params = pltpu.CompilerParams(vmem_limit_bytes=2**20)
+    return pl.pallas_call(mark_kernel, out_shape=out_shape, in_specs=[smem], out_specs=smem, compiler_params=params)(number)
+
+
+def final_kernel(line_ref, *refs):
+    pieces, inverse_ref, out_ref, joined = refs[:-3], refs[-3], refs[-2], refs[-1]
+    lines, halves, chunk = len(pieces), pieces[0].shape[0], pieces[0].shape[1]
+    for number, piece in enumerate(pieces):
+        for half in range(halves):
+            at = (number * halves + half) * chunk
+            joined[at : at + chunk, :] = piece[half]
+
+    def block(pair, carry):
+        start = pl.multiple_of(pair * 2 * halves * chunk, 2 * halves * chunk)
+        product = dot(joined[pl.ds(start, 2 * halves * chunk), :], inverse_ref[...], ((1,), (1,)))
+        for step in range(2):
+            sender = (line_ref[0] + (lines - 2 * pair - step)) % lines
+            for half in range(halves):
+                at = (step * halves + half) * chunk
+                there = pl.ds(pl.multiple_of((half * lines + sender) * chunk, chunk), chunk)
+                out_ref[there, :] = -product[at : at + chunk, :]
+        return carry
+
+    lax.fori_loop(0, lines // 2, block, 0)
+
+
 def scratch(pieces, chunk, orbs):
     wide = pieces * chunk
     return [
@@ -271,29 +312,23 @@
     return jnp.sum(lax.all_to_all(parts, axes, 0, 0, tiled=True), axis=0)
 
 
-def packed(rows, coords):
-    return jnp.concatenate([rows, jnp.pad(coords, ((0, 5), (0, rows.shape[1] - coords.shape[1])))], axis=0)
-
-
 def shards(orbitals, points):
     rows, orbs = orbitals.shape
     core = lax.axis_index("c")
-    line, yh = lax.axis_index("x"), lax.axis_index("yh")
+    line = lax.axis_index("x")
     core_ref = core.astype(jnp.int32)[None]
-    place = [core_ref, line.astype(jnp.int32)[None], yh.astype(jnp.int32)[None]]
+    place = [core_ref, line.astype(jnp.int32)[None]]
     groups = lax.axis_size(("yh", "x"))
     group = lax.axis_index(("yh", "x"))
     chunk = rows // groups
     weight = 1.0 / (rows * lax.axis_size(("yl", "z", "c")))
-    barrier = lax.optimization_barrier
-
-    own = packed(
-        lax.dynamic_slice_in_dim(orbitals, group * chunk, chunk, 0),
-        lax.dynamic_slice_in_dim(points, group * chunk, chunk, 1),
-    )
+
     middle = rows // 2
-    from_below = shift_y(packed(orbitals[:middle], points[:, :middle]), 1)
-    from_above = shift_y(packed(orbitals[middle:], points[:, middle:]), -1)
+    message = [jax.ShapeDtypeStruct((size + 8, orbs), jnp.float32) for size in (chunk, middle, middle)]
+    group_ref = group.astype(jnp.int32)[None]
+    own, lower_half, upper_half = call(pack_kernel, tuple(message), [], {}, 10**8, 3, group_ref, *place, orbitals, points)
+    from_below = shift_y(lower_half, 1)
+    from_above = shift_y(upper_half, -1)
     far = {0: own}
     ring = lax.axis_size("z")
     order = [0]
@@ -308,7 +343,7 @@
     turned_type = jax.ShapeDtypeStruct((orbs, 3 * tall), jnp.bfloat16)
     spread_type = jax.ShapeDtypeStruct((3, tall, SIDE), jnp.float32)
     near, turned, spread = call(
-        near_kernel, (near_type, turned_type, spread_type), [], {}, 10**9, 3, *place, orbitals, points, from_below, from_above
+        near_kernel, (near_type, turned_type, spread_type), [], {}, 10**9, 0, lower_half, upper_half, from_below, from_above
     )
     total_type = jax.ShapeDtypeStruct((tall, orbs), jnp.float32)
     stages = [order[:3], order[3:5], order[5:7], order[7:]]
@@ -339,8 +374,6 @@
     to_below = shift_y(to_below, -1)
     plane = lax.axis_size(PLANE)
     piece = scattered_sum(half.reshape(plane, -1, SIDE), PLANE)
-    piece, to_above, to_below = barrier((piece, to_above, to_below))
-
     applied = own_part + jnp.concatenate([to_above, to_below], axis=0)
     lines = lax.axis_size("x")
     by_line = applied.reshape(groups // lines, lines, chunk, orbs)
@@ -350,16 +383,20 @@
         parts.append(shift(part, "x", distance))
     piece = jnp.sum(gathered(piece, "z"), axis=0)
     pair = sum(parts[1:], parts[0])
-    kept = lax.dynamic_index_in_dim(pair, yh, 0, keepdims=False)
-    sent = shift(lax.dynamic_index_in_dim(pair, 1 - yh, 0, keepdims=False), "yh", 1)
-
+    other_pair = shift(pair, "yh", 1)
     half = gathered(piece, PLANE).reshape(-1, SIDE)
-    half, kept, sent = barrier((half, kept, sent))
-    applied = kept + sent
-    far_half, applied = barrier((shift(half, "c", 1), applied))
-    applied = gathered(applied, ("yh", "x")).reshape(rows, orbs)
+    pair = pair + other_pair
+    held = [pair]
+    for distance in range(1, lines):
+        held.append(shift(pair, "x", distance))
+    line_ref = place[1]
+    for _ in range(3):
+        line_ref = mark(line_ref)
+    far_half = shift(half, "c", 1)
     inverse = chol_inverse(core_ref, half, far_half, orbs)
-    return -dot(applied, inverse, ((1,), (1,)))
+    out_type = jax.ShapeDtypeStruct((rows, orbs), jnp.float32)
+    final_scratch = [pltpu.VMEM((rows, orbs), jnp.float32)]
+    return call(final_kernel, out_type, final_scratch, {}, 10**9, 1, line_ref, *held, inverse)
 
 
 def solution(mesh):

time: 142 us -> 152 us (1.070); the launches traced: 142 us -> 149 us
  blocking collectives: 0 us -> 15 us
  Pallas kernels: 36.1 us -> 41.5 us
  waiting for transfers between devices: 25.9 us -> 20.8 us
  matrix products: 2.83 us -> 0 us
  other arithmetic: 2.8 us -> 0.41 us
  starting transfers between devices: 70.1 us -> 68 us
    all_to_all x0 -> x1, blocking collectives: none -> 15 us  [scattered_sum(): return jnp.sum(lax.all_to_all(parts, axes, 0, 0, tiled=True), axis=0)]
    all_to_all x1 -> x0, waiting for transfers between devices: 10.1 us -> none  [scattered_sum(): return jnp.sum(lax.all_to_all(parts, axes, 0, 0, tiled=True), axis=0)]
    ppermute x21 -> x24, starting transfers between devices: 44.7 us -> 51.3 us  [shift(): lax.ppermute(block, axis, [(i, (i + distance) % size) for i in range(size)])]
    all_to_all x3 -> x2, waiting for transfers between devices: 4.15 us -> 10.7 us  [gathered(): return lax.all_to_all(copies, axes, 0, 0, tiled=True)]
    all_to_all x3 -> x2, starting transfers between devices: 15 us -> 10.2 us  [gathered(): return lax.all_to_all(copies, axes, 0, 0, tiled=True)]
    all_to_all x1 -> x0, starting transfers between devices: 4.13 us -> none  [scattered_sum(): return jnp.sum(lax.all_to_all(parts, axes, 0, 0, tiled=True), axis=0)]
    dot_general x1 -> x0, matrix products: 2.83 us -> none  [dot(): lax.dot_general(a, b, (dims, ((), ())), precision=precision, preferred_el...]
    pallas_call x0 -> x3, Pallas kernels: none -> 2.8 us  [mark(): pl.pallas_call(mark_kernel, out_shape=out_shape, in_specs=[smem], out_spe...]
  transfers between devices with their start and end apart: 29 -> 30, of which waited for: 8 -> 7; matrix products, arithmetic and copies ran while one was open for 2% -> 1% of each run, Pallas kernels for 21% -> 21%
where the time goes in v2:
time: 152 us; the launch traced here: 149 us
  starting transfers between devices  68 us (45%)
  Pallas kernels  41.5 us (27%)
  waiting for transfers between devices  20.8 us (14%)
  blocking collectives  15 us (10%)
  local copies, waits for them, and re-layouts  3.43 us (2%)
    ppermute x24, starting transfers between devices, shift(): lax.ppermute(block, axis, [(i, (i + distance) % size) for i in range(size)])  51.3 us
    pallas_call x8, Pallas kernels, call(): pl.pallas_call(body, out_shape=out_shape, in_specs=[smem] * scalars + [vm...  38.7 us
    all_to_all x1, blocking collectives, scattered_sum(): return jnp.sum(lax.all_to_all(parts, axes, 0, 0, tiled=True), axis=0)  15 us
    all_to_all x2, waiting for transfers between devices, gathered(): return lax.all_to_all(copies, axes, 0, 0, tiled=True)  10.7 us
    all_to_all x2, starting transfers between devices, gathered(): return lax.all_to_all(copies, axes, 0, 0, tiled=True)  10.2 us
    ppermute x24, waiting for transfers between devices, shift(): lax.ppermute(block, axis, [(i, (i + distance) % size) for i in range(size)])  10 us
    ppermute x4, starting transfers between devices, shift_y(): lax.ppermute(block, ('yl', 'yh'), [(place[y], place[(y + distance) % size...  6.4 us
  transfers between devices with their start and end apart: 30, of which 7 were waited for; matrix products, arithmetic and copies ran while one was open for 1% of the time, Pallas kernels for 21%

profile of v2, /device:TPU:1, one launch (start us, length us, event | category | flops | bytes accessed | tf_op | source)
XLA Modules:
  0.0 149.4 jit_solution(9489362818626344046)
XLA Ops:
  2.1 2.2 %collective-permute-start = (f32[264,512]{1,0:T(8,128)S(1)}, f32[264,512]{1,0:T(8,128)S(1)}, u32[]{:S(2)}, u32[]{:S(2)}) collective-permute-start(f32[264,512]{1,0:T(8,128)S(1)} %get-tuple-element.16.lower_ref), channel_id=1, source_target_pairs={{0,128},{128,4},{4,132},{132,0},{1,129},{129,5},{5,133},{133,1},{2... | collective-permute-start | bytes 1622024 | tf_op jit(solution)/shard_map/ppermute | solution.py:303
  7.4 3.9 %collective-permute-start.5 = (f32[72,512]{1,0:T(8,128)S(1)}, f32[72,512]{1,0:T(8,128)S(1)}, u32[]{:S(2)}, u32[]{:S(2)}) collective-permute-start(f32[72,512]{1,0:T(8,128)S(1)} %get-tuple-element.21.refs_2_), channel_id=1, source_target_pairs={{0,112},{16,0},{32,16},{48,32},{64,48},{80,64},{96,80},{112,96},{1... | collective-permute-start | bytes 442376 | tf_op jit(solution)/shard_map/ppermute | solution.py:297
  16.9 1.8 %collective-permute-start.11 = (f32[72,512]{1,0:T(8,128)S(1)}, f32[72,512]{1,0:T(8,128)S(1)}, u32[]{:S(2)}, u32[]{:S(2)}) collective-permute-start(f32[72,512]{1,0:T(8,128)S(1)} %get-tuple-element.21.refs_2_), channel_id=1, source_target_pairs={{0,48},{16,64},{32,80},{48,96},{64,112},{80,0},{96,16},{112,32},{1... | collective-permute-start | bytes 442376 | tf_op jit(solution)/shard_map/ppermute | solution.py:297
  18.7 4.6 %collective-permute-done.9.refs_5_ = f32[72,512]{1,0:T(8,128)S(1)} collective-permute-done((f32[72,512]{1,0:T(8,128)S(1)}, f32[72,512]{1,0:T(8,128)S(1)}, u32[]{:S(2)}, u32[]{:S(2)}) %collective-permute-start.9) | collective-permute-done | bytes 147488 | tf_op jit(solution)/shard_map/ppermute | solution.py:297
  24.2 2.3 %collective-permute-start.15 = (f32[72,512]{1,0:T(8,128)S(1)}, f32[72,512]{1,0:T(8,128)S(1)}, u32[]{:S(2)}, u32[]{:S(2)}) collective-permute-start(f32[72,512]{1,0:T(8,128)S(1)} %get-tuple-element.21.refs_2_), channel_id=1, source_target_pairs={{0,64},{16,80},{32,96},{48,112},{64,0},{80,16},{96,32},{112,48},{1... | collective-permute-start | bytes 442376 | tf_op jit(solution)/shard_map/ppermute | solution.py:297
  26.5 12.4 %collective-permute-start.4 = (f32[72,512]{1,0:T(8,128)S(1)}, f32[72,512]{1,0:T(8,128)S(1)}, u32[]{:S(2)}, u32[]{:S(2)}) collective-permute-start(f32[72,512]{1,0:T(8,128)S(1)} %collective-permute-done.3.refs_4_), channel_id=1, source_target_pairs={{0,8},{8,0},{1,9},{9,1},{2,10},{10,2},{3,11},{11,3},{4,12},{12,4},... | collective-permute-start | bytes 442376 | tf_op jit(solution)/shard_map/ppermute | solution.py:297
  40.9 4.5 %collective-permute-start.12 = (f32[72,512]{1,0:T(8,128)S(1)}, f32[72,512]{1,0:T(8,128)S(1)}, u32[]{:S(2)}, u32[]{:S(2)}) collective-permute-start(f32[72,512]{1,0:T(8,128)S(1)} %collective-permute-done.11.refs_3_), channel_id=1, source_target_pairs={{0,8},{8,0},{1,9},{9,1},{2,10},{10,2},{3,11},{11,3},{4,12},{12,4},... | collective-permute-start | bytes 442376 | tf_op jit(solution)/shard_map/ppermute | solution.py:297
  45.9 3.5 %shard_map.33.refs_2_ = f32[1024,512]{1,0:T(8,128)S(1)} custom-call(bf16[1024,1536]{1,0:T(8,128)(2,1)S(1)} %get-tuple-element.18.refs_0_.near_ref, f32[3,1024,128]{2,1,0:T(8,128)S(1)} %get-tuple-element.19.refs_1_.spread_ref, f32[72,512]{1,0:T(8,128)S(1)} %get-tuple-element.21.refs_2_, f32[72,512]{1,0:T(8,128)S(1)} %collective-permute-done.2.refs_3_, ...), custom_call_target="tpu_custom_call" | custom-call | flops 4000000000 | bytes 2000000 | tf_op jit(solution)/shard_map/pallas_call | solution.py:128
  49.4 3.4 %shard_map.34.refs_2_ = f32[1024,512]{1,0:T(8,128)S(1)} custom-call(bf16[1024,1536]{1,0:T(8,128)(2,1)S(1)} %get-tuple-element.18.refs_0_.near_ref, f32[3,1024,128]{2,1,0:T(8,128)S(1)} %get-tuple-element.19.refs_1_.spread_ref, f32[1024,512]{1,0:T(8,128)S(1)} %shard_map.33.refs_2_, ...), custom_call_target="tpu_custom_call", output_to_operand_aliasing={{}: (2, {})} | custom-call | flops 3000000000 | bytes 2000000 | tf_op jit(solution)/shard_map/pallas_call | solution.py:128
  52.8 3.4 %shard_map.35.acc = f32[1024,512]{1,0:T(8,128)S(1)} custom-call(bf16[1024,1536]{1,0:T(8,128)(2,1)S(1)} %get-tuple-element.18.refs_0_.near_ref, f32[3,1024,128]{2,1,0:T(8,128)S(1)} %get-tuple-element.19.refs_1_.spread_ref, f32[1024,512]{1,0:T(8,128)S(1)} %shard_map.34.refs_2_, ...), custom_call_target="tpu_custom_call", output_to_operand_aliasing={{}: (2, {})} | custom-call | flops 3000000000 | bytes 2000000 | tf_op jit(solution)/shard_map/pallas_call | solution.py:128
  56.2 5.5 %shard_map.36 = (f32[512,512]{1,0:T(8,128)S(1)}, f32[256,512]{1,0:T(8,128)S(1)}, f32[256,512]{1,0:T(8,128)S(1)}, f32[640,128]{1,0:T(8,128)S(1)}, f32[640,128]{1,0:T(8,128)S(1)}) custom-call(s32[1]{0:T(128)} %bitcast.1.core_ref, bf16[1024,1536]{1,0:T(8,128)(2,1)S(1)} %get-tuple-element.18.refs_0_.near_ref, ...), custom_call_target="tpu_custom_call" | custom-call | flops 3000000000 | bytes 2000000 | tf_op jit(solution)/shard_map/pallas_call | solution.py:128
  62.0 2.7 %collective-permute-start.18 = (f32[256,512]{1,0:T(8,128)S(1)}, f32[256,512]{1,0:T(8,128)S(1)}, u32[]{:S(2)}, u32[]{:S(2)}) collective-permute-start(f32[256,512]{1,0:T(8,128)S(1)} %get-tuple-element.24), channel_id=1, source_target_pairs={{0,132},{128,0},{4,128},{132,4},{1,133},{129,1},{5,129},{133,5},{2... | collective-permute-start | bytes 1572872 | tf_op jit(solution)/shard_map/ppermute | solution.py:303
  64.8 15.0 %all_to_all.15 = f32[16,40,128]{2,1,0:T(8,128)S(1)} all-to-all(f32[16,40,128]{2,1,0:T(8,128)S(1)} %bitcast.30), channel_id=1, replica_groups=mesh['yl'=2,'z'=8,'c'=2,'yh'=2,'x'=4] {'x','yh','yl'}, dimensions={0} | all-to-all | bytes 655360 | tf_op jit(solution)/shard_map/all_to_all | solution.py:312
  80.5 4.1 %all-to-all-start.1 = ((f32[8,40,128]{2,1,0:T(8,128)}), f32[8,40,128]{2,1,0:T(8,128)S(1)}, u32[]{:S(2)}, u32[]{:S(2)}) async-start(f32[8,40,128]{2,1,0:T(8,128)} %broadcast_in_dim.24), calls=%async_computation.1 | async-start | bytes 327680 | tf_op jit(solution)/shard_map/all_to_all | solution.py:308
  84.8 8.1 %all-to-all-done.1 = f32[8,40,128]{2,1,0:T(8,128)S(1)} async-done(((f32[8,40,128]{2,1,0:T(8,128)}), f32[8,40,128]{2,1,0:T(8,128)S(1)}, u32[]{:S(2)}, u32[]{:S(2)}) %all-to-all-start.1) | async-done | bytes 163872 | tf_op jit(solution)/shard_map/all_to_all | solution.py:308
  93.7 6.2 %all-to-all-start.2 = ((f32[16,40,128]{2,1,0:T(8,128)}), f32[16,40,128]{2,1,0:T(8,128)S(1)}, u32[]{:S(2)}, u32[]{:S(2)}) async-start(f32[16,40,128]{2,1,0:T(8,128)} %broadcast_in_dim.25), calls=%async_computation.2 | async-start | bytes 655360 | tf_op jit(solution)/shard_map/all_to_all | solution.py:308
  101.4 2.4 %collective-permute-start.20 = (f32[2,64,512]{2,1,0:T(8,128)S(1)}, f32[2,64,512]{2,1,0:T(8,128)S(1)}, u32[]{:S(2)}, u32[]{:S(2)}) collective-permute-start(f32[2,64,512]{2,1,0:T(8,128)S(1)} %get-tuple-element.28), channel_id=1, source_target_pairs={{0,2},{1,3},{2,0},{3,1},{4,6},{5,7},{6,4},{7,5},{8,10},{9,11},{10,... | collective-permute-start | bytes 786440 | tf_op jit(solution)/shard_map/ppermute | solution.py:297
  105.0 2.6 %all-to-all-done.2 = f32[16,40,128]{2,1,0:T(8,128)S(1)} async-done(((f32[16,40,128]{2,1,0:T(8,128)}), f32[16,40,128]{2,1,0:T(8,128)S(1)}, u32[]{:S(2)}, u32[]{:S(2)}) %all-to-all-start.2) | async-done | bytes 327712 | tf_op jit(solution)/shard_map/all_to_all | solution.py:308
  107.6 5.6 %collective-permute-start.27 = (f32[640,128]{1,0:T(8,128)S(1)}, f32[640,128]{1,0:T(8,128)S(1)}, u32[]{:S(2)}, u32[]{:S(2)}) collective-permute-start(f32[640,128]{1,0:T(8,128)S(1)} %bitcast.26), channel_id=1, source_target_pairs={{0,8},{8,0},{1,9},{9,1},{2,10},{10,2},{3,11},{11,3},{4,12},{12,4},... | collective-permute-start | bytes 983048 | tf_op jit(solution)/shard_map/ppermute | solution.py:297
  115.0 3.3 %collective-permute-start.22 = (f32[2,64,512]{2,1,0:T(8,128)S(1)}, f32[2,64,512]{2,1,0:T(8,128)S(1)}, u32[]{:S(2)}, u32[]{:S(2)}) collective-permute-start(f32[2,64,512]{2,1,0:T(8,128)S(1)} %fusion.1), channel_id=1, source_target_pairs={{0,4},{4,0},{1,5},{5,1},{2,6},{6,2},{3,7},{7,3},{8,12},{12,8},{9,1... | collective-permute-start | bytes 786440 | tf_op jit(solution)/shard_map/ppermute | solution.py:297
  122.1 2.8 %collective-permute-start.23 = (f32[2,64,512]{2,1,0:T(8,128)S(1)}, f32[2,64,512]{2,1,0:T(8,128)S(1)}, u32[]{:S(2)}, u32[]{:S(2)}) collective-permute-start(f32[2,64,512]{2,1,0:T(8,128)S(1)} %add.68.refs_0_), channel_id=1, source_target_pairs={{0,1},{1,2},{2,3},{3,0},{4,5},{5,6},{6,7},{7,4},{8,9},{9,10},{10,1... | collective-permute-start | bytes 786440 | tf_op jit(solution)/shard_map/ppermute | solution.py:297
  124.9 2.8 %collective-permute-start.24 = (f32[2,64,512]{2,1,0:T(8,128)S(1)}, f32[2,64,512]{2,1,0:T(8,128)S(1)}, u32[]{:S(2)}, u32[]{:S(2)}) collective-permute-start(f32[2,64,512]{2,1,0:T(8,128)S(1)} %add.68.refs_0_), channel_id=1, source_target_pairs={{0,2},{1,3},{2,0},{3,1},{4,6},{5,7},{6,4},{7,5},{8,10},{9,11},{10,... | collective-permute-start | bytes 786440 | tf_op jit(solution)/shard_map/ppermute | solution.py:297
  127.7 17.8 %shard_map.37.refs_4_ = f32[512,512]{1,0:T(8,128)S(1)} custom-call(s32[1]{0:T(128)} %bitcast.1.core_ref, f32[640,128]{1,0:T(8,128)S(1)} %bitcast.27, f32[640,128]{1,0:T(8,128)S(1)} %collective-permute-done.27.other_ref), custom_call_target="tpu_custom_call" | custom-call | flops 20000000000 | bytes 2000000 | tf_op jit(solution)/shard_map/pallas_call | solution.py:128
  145.6 3.8 %shard_map.38 = f32[512,512]{1,0:T(8,128)} custom-call(s32[1]{0:T(128)} %shard_map.30.line_ref, f32[2,64,512]{2,1,0:T(8,128)S(1)} %add.68.refs_0_, f32[2,64,512]{2,1,0:T(8,128)S(1)} %collective-permute-done.23.refs_1_, f32[2,64,512]{2,1,0:T(8,128)S(1)} %collective-permute-done.24.refs_2_, f32[2,64,512]{2,1,0:T(8,128)S(1)} %collective-permute-done.25.refs_3_, ...), custom_call_target="tpu_custom_call" | custom-call | flops 1000000000 | bytes 2000000 | tf_op jit(solution)/shard_map/pallas_call | solution.py:128
  (61 shorter events, 24.6 us)
Async XLA Ops:
  2.1 24.4 %collective-permute-start = (f32[264,512]{1,0:T(8,128)S(1)}, f32[264,512]{1,0:T(8,128)S(1)}, u32[]{:S(2)}, u32[]{:S(2)}) collective-permute-start(f32[264,512]{1,0:T(8,128)S(1)} %get-tuple-element.16.lower_ref), channel_id=1, source_target_pairs={{0,128},{128,4},{4,132},{132,0},{1,129},{129,5},{5,133},{133,1},{2... | collective-permute-start | bytes 1622024 | tf_op jit(solution)/shard_map/ppermute | solution.py:303
  4.3 34.6 %collective-permute-start.1 = (f32[264,512]{1,0:T(8,128)S(1)}, f32[264,512]{1,0:T(8,128)S(1)}, u32[]{:S(2)}, u32[]{:S(2)}) collective-permute-start(f32[264,512]{1,0:T(8,128)S(1)} %get-tuple-element.17.upper_ref), channel_id=1, source_target_pairs={{0,132},{128,0},{4,128},{132,4},{1,133},{129,1},{5,129},{133,5},{2... | collective-permute-start | bytes 1622024 | tf_op jit(solution)/shard_map/ppermute | solution.py:303
  5.8 8.7 %collective-permute-start.3 = (f32[72,512]{1,0:T(8,128)S(1)}, f32[72,512]{1,0:T(8,128)S(1)}, u32[]{:S(2)}, u32[]{:S(2)}) collective-permute-start(f32[72,512]{1,0:T(8,128)S(1)} %get-tuple-element.21.refs_2_), channel_id=1, source_target_pairs={{0,16},{16,32},{32,48},{48,64},{64,80},{80,96},{96,112},{112,0},{1... | collective-permute-start | bytes 442376 | tf_op jit(solution)/shard_map/ppermute | solution.py:297
  7.4 8.7 %collective-permute-start.5 = (f32[72,512]{1,0:T(8,128)S(1)}, f32[72,512]{1,0:T(8,128)S(1)}, u32[]{:S(2)}, u32[]{:S(2)}) collective-permute-start(f32[72,512]{1,0:T(8,128)S(1)} %get-tuple-element.21.refs_2_), channel_id=1, source_target_pairs={{0,112},{16,0},{32,16},{48,32},{64,48},{80,64},{96,80},{112,96},{1... | collective-permute-start | bytes 442376 | tf_op jit(solution)/shard_map/ppermute | solution.py:297
  14.5 8.7 %collective-permute-start.9 = (f32[72,512]{1,0:T(8,128)S(1)}, f32[72,512]{1,0:T(8,128)S(1)}, u32[]{:S(2)}, u32[]{:S(2)}) collective-permute-start(f32[72,512]{1,0:T(8,128)S(1)} %get-tuple-element.21.refs_2_), channel_id=1, source_target_pairs={{0,96},{16,112},{32,0},{48,16},{64,32},{80,48},{96,64},{112,80},{1... | collective-permute-start | bytes 442376 | tf_op jit(solution)/shard_map/ppermute | solution.py:297
  16.9 23.4 %collective-permute-start.11 = (f32[72,512]{1,0:T(8,128)S(1)}, f32[72,512]{1,0:T(8,128)S(1)}, u32[]{:S(2)}, u32[]{:S(2)}) collective-permute-start(f32[72,512]{1,0:T(8,128)S(1)} %get-tuple-element.21.refs_2_), channel_id=1, source_target_pairs={{0,48},{16,64},{32,80},{48,96},{64,112},{80,0},{96,16},{112,32},{1... | collective-permute-start | bytes 442376 | tf_op jit(solution)/shard_map/ppermute | solution.py:297
  23.3 17.5 %collective-permute-start.13 = (f32[72,512]{1,0:T(8,128)S(1)}, f32[72,512]{1,0:T(8,128)S(1)}, u32[]{:S(2)}, u32[]{:S(2)}) collective-permute-start(f32[72,512]{1,0:T(8,128)S(1)} %get-tuple-element.21.refs_2_), channel_id=1, source_target_pairs={{0,80},{16,96},{32,112},{48,0},{64,16},{80,32},{96,48},{112,64},{1... | collective-permute-start | bytes 442376 | tf_op jit(solution)/shard_map/ppermute | solution.py:297
  24.2 16.7 %collective-permute-start.15 = (f32[72,512]{1,0:T(8,128)S(1)}, f32[72,512]{1,0:T(8,128)S(1)}, u32[]{:S(2)}, u32[]{:S(2)}) collective-permute-start(f32[72,512]{1,0:T(8,128)S(1)} %get-tuple-element.21.refs_2_), channel_id=1, source_target_pairs={{0,64},{16,80},{32,96},{48,112},{64,0},{80,16},{96,32},{112,48},{1... | collective-permute-start | bytes 442376 | tf_op jit(solution)/shard_map/ppermute | solution.py:297
  26.5 18.9 %collective-permute-start.4 = (f32[72,512]{1,0:T(8,128)S(1)}, f32[72,512]{1,0:T(8,128)S(1)}, u32[]{:S(2)}, u32[]{:S(2)}) collective-permute-start(f32[72,512]{1,0:T(8,128)S(1)} %collective-permute-done.3.refs_4_), channel_id=1, source_target_pairs={{0,8},{8,0},{1,9},{9,1},{2,10},{10,2},{3,11},{11,3},{4,12},{12,4},... | collective-permute-start | bytes 442376 | tf_op jit(solution)/shard_map/ppermute | solution.py:297
  40.2 9.1 %collective-permute-start.10 = (f32[72,512]{1,0:T(8,128)S(1)}, f32[72,512]{1,0:T(8,128)S(1)}, u32[]{:S(2)}, u32[]{:S(2)}) collective-permute-start(f32[72,512]{1,0:T(8,128)S(1)} %collective-permute-done.9.refs_5_), channel_id=1, source_target_pairs={{0,8},{8,0},{1,9},{9,1},{2,10},{10,2},{3,11},{11,3},{4,12},{12,4},... | collective-permute-start | bytes 442376 | tf_op jit(solution)/shard_map/ppermute | solution.py:297
  40.8 8.6 %collective-permute-start.8 = (f32[72,512]{1,0:T(8,128)S(1)}, f32[72,512]{1,0:T(8,128)S(1)}, u32[]{:S(2)}, u32[]{:S(2)}) collective-permute-start(f32[72,512]{1,0:T(8,128)S(1)} %collective-permute-done.7.refs_3_), channel_id=1, source_target_pairs={{0,8},{8,0},{1,9},{9,1},{2,10},{10,2},{3,11},{11,3},{4,12},{12,4},... | collective-permute-start | bytes 442376 | tf_op jit(solution)/shard_map/ppermute | solution.py:297
  40.9 11.9 %collective-permute-start.12 = (f32[72,512]{1,0:T(8,128)S(1)}, f32[72,512]{1,0:T(8,128)S(1)}, u32[]{:S(2)}, u32[]{:S(2)}) collective-permute-start(f32[72,512]{1,0:T(8,128)S(1)} %collective-permute-done.11.refs_3_), channel_id=1, source_target_pairs={{0,8},{8,0},{1,9},{9,1},{2,10},{10,2},{3,11},{11,3},{4,12},{12,4},... | collective-permute-start | bytes 442376 | tf_op jit(solution)/shard_map/ppermute | solution.py:297
  45.4 10.8 %collective-permute-start.16 = (f32[72,512]{1,0:T(8,128)S(1)}, f32[72,512]{1,0:T(8,128)S(1)}, u32[]{:S(2)}, u32[]{:S(2)}) collective-permute-start(f32[72,512]{1,0:T(8,128)S(1)} %collective-permute-done.15.refs_0_), channel_id=1, source_target_pairs={{0,8},{8,0},{1,9},{9,1},{2,10},{10,2},{3,11},{11,3},{4,12},{12,4},... | collective-permute-start | bytes 442376 | tf_op jit(solution)/shard_map/ppermute | solution.py:297
  62.0 22.5 %collective-permute-start.17 = (f32[256,512]{1,0:T(8,128)S(1)}, f32[256,512]{1,0:T(8,128)S(1)}, u32[]{:S(2)}, u32[]{:S(2)}) collective-permute-start(f32[256,512]{1,0:T(8,128)S(1)} %get-tuple-element.23), channel_id=1, source_target_pairs={{0,128},{128,4},{4,132},{132,0},{1,129},{129,5},{5,133},{133,1},{2... | collective-permute-start | bytes 1572872 | tf_op jit(solution)/shard_map/ppermute | solution.py:303
  62.0 22.5 %collective-permute-start.18 = (f32[256,512]{1,0:T(8,128)S(1)}, f32[256,512]{1,0:T(8,128)S(1)}, u32[]{:S(2)}, u32[]{:S(2)}) collective-permute-start(f32[256,512]{1,0:T(8,128)S(1)} %get-tuple-element.24), channel_id=1, source_target_pairs={{0,132},{128,0},{4,128},{132,4},{1,133},{129,1},{5,129},{133,5},{2... | collective-permute-start | bytes 1572872 | tf_op jit(solution)/shard_map/ppermute | solution.py:303
  80.5 12.4 %all-to-all-start.1 = ((f32[8,40,128]{2,1,0:T(8,128)}), f32[8,40,128]{2,1,0:T(8,128)S(1)}, u32[]{:S(2)}, u32[]{:S(2)}) async-start(f32[8,40,128]{2,1,0:T(8,128)} %broadcast_in_dim.24), calls=%async_computation.1 | async-start | bytes 327680 | tf_op jit(solution)/shard_map/all_to_all | solution.py:308
  93.7 13.9 %all-to-all-start.2 = ((f32[16,40,128]{2,1,0:T(8,128)}), f32[16,40,128]{2,1,0:T(8,128)S(1)}, u32[]{:S(2)}, u32[]{:S(2)}) async-start(f32[16,40,128]{2,1,0:T(8,128)} %broadcast_in_dim.25), calls=%async_computation.2 | async-start | bytes 655360 | tf_op jit(solution)/shard_map/all_to_all | solution.py:308
  100.0 13.2 %collective-permute-start.19 = (f32[2,64,512]{2,1,0:T(8,128)S(1)}, f32[2,64,512]{2,1,0:T(8,128)S(1)}, u32[]{:S(2)}, u32[]{:S(2)}) collective-permute-start(f32[2,64,512]{2,1,0:T(8,128)S(1)} %get-tuple-element.27), channel_id=1, source_target_pairs={{0,1},{1,2},{2,3},{3,0},{4,5},{5,6},{6,7},{7,4},{8,9},{9,10},{10,1... | collective-permute-start | bytes 786440 | tf_op jit(solution)/shard_map/ppermute | solution.py:297
  101.4 13.5 %collective-permute-start.20 = (f32[2,64,512]{2,1,0:T(8,128)S(1)}, f32[2,64,512]{2,1,0:T(8,128)S(1)}, u32[]{:S(2)}, u32[]{:S(2)}) collective-permute-start(f32[2,64,512]{2,1,0:T(8,128)S(1)} %get-tuple-element.28), channel_id=1, source_target_pairs={{0,2},{1,3},{2,0},{3,1},{4,6},{5,7},{6,4},{7,5},{8,10},{9,11},{10,... | collective-permute-start | bytes 786440 | tf_op jit(solution)/shard_map/ppermute | solution.py:297
  103.8 11.2 %collective-permute-start.21 = (f32[2,64,512]{2,1,0:T(8,128)S(1)}, f32[2,64,512]{2,1,0:T(8,128)S(1)}, u32[]{:S(2)}, u32[]{:S(2)}) collective-permute-start(f32[2,64,512]{2,1,0:T(8,128)S(1)} %get-tuple-element.29), channel_id=1, source_target_pairs={{0,3},{1,0},{2,1},{3,2},{4,7},{5,4},{6,5},{7,6},{8,11},{9,8},{10,9... | collective-permute-start | bytes 786440 | tf_op jit(solution)/shard_map/ppermute | solution.py:297
  107.6 20.1 %collective-permute-start.27 = (f32[640,128]{1,0:T(8,128)S(1)}, f32[640,128]{1,0:T(8,128)S(1)}, u32[]{:S(2)}, u32[]{:S(2)}) collective-permute-start(f32[640,128]{1,0:T(8,128)S(1)} %bitcast.26), channel_id=1, source_target_pairs={{0,8},{8,0},{1,9},{9,1},{2,10},{10,2},{3,11},{11,3},{4,12},{12,4},... | collective-permute-start | bytes 983048 | tf_op jit(solution)/shard_map/ppermute | solution.py:297
  122.1 23.4 %collective-permute-start.23 = (f32[2,64,512]{2,1,0:T(8,128)S(1)}, f32[2,64,512]{2,1,0:T(8,128)S(1)}, u32[]{:S(2)}, u32[]{:S(2)}) collective-permute-start(f32[2,64,512]{2,1,0:T(8,128)S(1)} %add.68.refs_0_), channel_id=1, source_target_pairs={{0,1},{1,2},{2,3},{3,0},{4,5},{5,6},{6,7},{7,4},{8,9},{9,10},{10,1... | collective-permute-start | bytes 786440 | tf_op jit(solution)/shard_map/ppermute | solution.py:297
  124.9 20.7 %collective-permute-start.24 = (f32[2,64,512]{2,1,0:T(8,128)S(1)}, f32[2,64,512]{2,1,0:T(8,128)S(1)}, u32[]{:S(2)}, u32[]{:S(2)}) collective-permute-start(f32[2,64,512]{2,1,0:T(8,128)S(1)} %add.68.refs_0_), channel_id=1, source_target_pairs={{0,2},{1,3},{2,0},{3,1},{4,6},{5,7},{6,4},{7,5},{8,10},{9,11},{10,... | collective-permute-start | bytes 786440 | tf_op jit(solution)/shard_map/ppermute | solution.py:297
  127.7 17.9 %collective-permute-start.25 = (f32[2,64,512]{2,1,0:T(8,128)S(1)}, f32[2,64,512]{2,1,0:T(8,128)S(1)}, u32[]{:S(2)}, u32[]{:S(2)}) collective-permute-start(f32[2,64,512]{2,1,0:T(8,128)S(1)} %add.68.refs_0_), channel_id=1, source_target_pairs={{0,3},{1,0},{2,1},{3,2},{4,7},{5,4},{6,5},{7,6},{8,11},{9,8},{10,9... | collective-permute-start | bytes 786440 | tf_op jit(solution)/shard_map/ppermute | solution.py:297
  (8 other events, 39.4 us)
